TPU v7x, 512 devices: a whole 4x8x8 slice. The times are simulated.
512 devices in a mesh: kz: 16 (over x, z_hi), gx: 32 (over y, z_lo, core).
Axes of the slice: x: 4, y: 8, z: 8 (z_hi: 4, z_lo: 2; z = z_hi * 2 + z_lo), core: 2. Of those that a mesh axis runs over, the one named last changes fastest.
Arguments:
- kspace_lines: bfloat16 [16, 16, 128, 2, 512], P(None, 'kz', 'gx'), may hold values from -6 to 6
- acquired_at: int32 [16, 128], P('kz'), may hold values from 0 to 5
- ky_start: int32 [6], replicated, may hold values from -2 to 0, as said below
- kz_start: int32 [6], replicated, may hold values from -1 to 0, as said below
- kernels: bfloat16 [2, 6, 16, 6, 32], replicated, may hold values from -0.3125 to 0.3125
Outputs:
- filled: bfloat16 [2, 512, 16, 32, 384], P(None, 'gx', None, 'kz')
Inputs may be any that keep to these rules, and one draw needn't show every extreme that they name: acquired_at[b, a] = 2 ry + rz names the acquired position of the cell, with ky = 3 a + ry and kz = 2 b + rz. `ky_start`: each of -2, -1 and 0 appears exactly twice. `kz_start`: each of -1 and 0 appears exactly three times.
All inputs are finite; a program needn't handle non-finite values.
Results may differ from a plain program's by a relative error of at most 0.0057.
Values may be sent and summed in bfloat16 or wider, within the bound.
No kernel may reach another device: no remote copies, remote signals or barrier semaphores. Data moves between devices by JAX's collectives and lax.ppermute only.
A program may use at most 64 MiB of HBM per device.

v0:
```python
import math

import jax
import jax.numpy as jnp
from jax import lax
from jax.sharding import PartitionSpec as P


def with_halo(cells, sides, width):
    for axis, dim in sides:
        count = lax.axis_size(axis)
        ends = count - 1
        head = lax.slice_in_dim(cells, 0, width, axis=dim)
        tail = lax.slice_in_dim(cells, cells.shape[dim] - width, cells.shape[dim], axis=dim)
        cells = jnp.concatenate(
            [
                lax.ppermute(tail, axis, [(i, (i + 1) % count) for i in range(ends)]),
                cells,
                lax.ppermute(head, axis, [((i + 1) % count, i) for i in range(ends)]),
            ],
            axis=dim,
        )
    return cells


def readout_matrix(extent):
    wave_index = jnp.arange(extent, dtype=jnp.int32)
    phase_angle = (wave_index[:, None] * wave_index[None, :] % extent).astype(jnp.float32) * (
        2.0 * math.pi / extent
    )
    cosine = jnp.cos(phase_angle) / math.sqrt(extent)
    sine_part = jnp.sin(phase_angle) / math.sqrt(extent)
    from_real = jnp.stack([cosine, sine_part], axis=1)
    from_imag = jnp.stack([-sine_part, cosine], axis=1)
    return jnp.stack([from_real, from_imag], axis=0).astype(jnp.bfloat16)


def conjugate_flip(blocks):
    flipped = blocks[:, :, :, ::-1, ::-1]
    return jnp.concatenate([flipped[0:1], -flipped[1:2]], axis=0)


def complex_weights(kernels):
    real_part = kernels[0]
    imag_part = kernels[1]
    to_real = jnp.stack([real_part, -imag_part], axis=3)
    to_imag = jnp.stack([imag_part, real_part], axis=3)
    return jnp.stack([to_real, to_imag], axis=1)


def fill_grid(padded, actual, weights, acquired_at, ky_start, kz_start):
    kz_cells = actual.shape[3]
    ky_cells = actual.shape[4]
    filled = []
    for target in range(6):
        pieces = []
        for kz_point in range(2):
            kz_from = kz_start[target] + 1 + kz_point
            plane_rows = lax.dynamic_slice_in_dim(padded, kz_from, kz_cells, axis=3)
            for ky_point in range(3):
                ky_from = ky_start[target] + 2 + ky_point
                pieces.append(lax.dynamic_slice_in_dim(plane_rows, ky_from, ky_cells, axis=4))
        source = jnp.stack(pieces, axis=0)
        estimate = jnp.einsum(
            "scpqh,pqxhba->sxcba", weights[target], source, preferred_element_type=jnp.float32
        )
        chosen = jnp.where(acquired_at == target, actual.astype(jnp.float32), estimate)
        filled.append(chosen.astype(jnp.bfloat16))
    stacked = jnp.stack(filled, axis=0).reshape((3, 2) + actual.shape)
    reordered = jnp.transpose(stacked, (2, 3, 4, 5, 1, 6, 0))
    return reordered.reshape(
        actual.shape[0], actual.shape[1], actual.shape[2], 2 * kz_cells, 3 * ky_cells
    )


def local(kspace_lines, acquired_at, ky_start, kz_start, kernels):
    spectra = jnp.einsum(
        "cbaqk,qksx->sxcba",
        kspace_lines,
        readout_matrix(kspace_lines.shape[4]),
        preferred_element_type=jnp.float32,
    ).astype(jnp.bfloat16)
    planes = lax.all_to_all(spectra, "gx", split_axis=1, concat_axis=4, tiled=True)
    kz_slabs = lax.all_to_all(planes, "kz", split_axis=2, concat_axis=3, tiled=True)
    virtual = lax.all_to_all(
        conjugate_flip(kz_slabs), "kz", split_axis=3, concat_axis=2, tiled=True
    )
    channels = jnp.concatenate([planes, virtual], axis=2)
    padded = with_halo(channels, (("kz", 3),), 1)
    padded = jnp.pad(padded, ((0, 0), (0, 0), (0, 0), (0, 0), (2, 2)))
    return fill_grid(padded, planes, complex_weights(kernels), acquired_at, ky_start, kz_start)


def solution(mesh):
    placed = (P(None, "kz", "gx", None, None), P("kz", None), P(), P(), P())
    return jax.shard_map(
        local,
        mesh=mesh,
        in_specs=placed,
        out_specs=P(None, "gx", None, "kz", None),
        check_vma=False,
    )
```

profile of v0, /device:TPU:1, one launch (start us, length us, event | category | flops | bytes accessed | tf_op | source)
XLA Modules:
  0.0 137.9 jit_solution(17134937163343659161)
XLA Ops:
  0.0 4.0 %fusion.116 = bf16[512,1,512]{2,0,1:T(8,128)(2,1)S(1)} fusion(), kind=kLoop, calls=%fused_computation.69 | loop fusion | flops 4194304 | bytes 524288 | tf_op jit(solution)/shard_map/convert.7
  4.0 4.4 %negate_convert_fusion = (bf16[512,1,512]{2,0,1:T(8,128)(2,1)S(1)}, bf16[512,1,512]{2,0,1:T(8,128)(2,1)S(1)}) fusion(), kind=kLoop, calls=%fused_computation.63 | loop fusion | flops 4980736 | bytes 1048576 | tf_op jit(solution)/shard_map/convert.3
  8.6 0.7 copy-done.4
  9.3 0.4 fusion.73
  9.7 0.7 copy.111
  10.4 1.1 reshape.302
  11.6 19.6 %all_to_all.39 = bf16[32,2,1024]{2,1,0:T(2,128)(2,1)S(1)} all-to-all(bf16[32,2,1024]{2,1,0:T(2,128)(2,1)S(1)} %reshape.302), channel_id=1, replica_groups=mesh['kz'=16,'gx'=32] {'gx'}, dimensions={0} | all-to-all | bytes 262144 | tf_op jit(solution)/shard_map/all_to_all | solution.py:83
  31.2 0.7 reshape.303
  31.9 0.3 copy.174
  32.2 1.6 %copy.115 = bf16[2,16,16,1,128]{4,1,3,0,2:T(8,128)(2,1)} copy(bf16[2,16,16,1,128]{2,1,4,0,3:T(8,128)(2,1)S(1)} %bitcast.445) | data formatting | bytes 262144 | tf_op jit(solution)/shard_map/all_to_all | solution.py:83
  33.7 11.8 %all-to-all-start.1 = ((bf16[2,16,16,1,128]{4,1,3,0,2:T(8,128)(2,1)}), bf16[2,16,16,1,128]{4,1,3,0,2:T(8,128)(2,1)S(1)}, u32[]{:S(2)}, u32[]{:S(2)}) async-start(bf16[2,16,16,1,128]{4,1,3,0,2:T(8,128)(2,1)} %copy.115), calls=%async_computation.1 | async-start | bytes 262144 | tf_op jit(solution)/shard_map/all_to_all | solution.py:84
  45.6 9.5 %all-to-all-done.1 = bf16[2,16,16,1,128]{4,1,3,0,2:T(8,128)(2,1)S(1)} async-done(((bf16[2,16,16,1,128]{4,1,3,0,2:T(8,128)(2,1)}), bf16[2,16,16,1,128]{4,1,3,0,2:T(8,128)(2,1)S(1)}, u32[]{:S(2)}, u32[]{:S(2)}) %all-to-all-start.1) | async-done | bytes 131104 | tf_op jit(solution)/shard_map/all_to_all | solution.py:84
  55.4 0.7 copy.117
  56.0 3.5 %all-to-all-start.2 = ((bf16[2,16,1,16,128]{4,1,2,0,3:T(8,128)(2,1)}), bf16[2,16,1,16,128]{4,1,2,0,3:T(8,128)(2,1)S(1)}, u32[]{:S(2)}, u32[]{:S(2)}) async-start(bf16[2,16,1,16,128]{4,1,2,0,3:T(8,128)(2,1)} %copy.117), calls=%async_computation.2 | async-start | bytes 262144 | tf_op jit(solution)/shard_map/all_to_all | solution.py:85
  59.6 0.7 fusion.146
  60.4 0.8 copy.118
  61.2 8.1 %all-to-all-done.2 = bf16[2,16,1,16,128]{4,1,2,0,3:T(8,128)(2,1)S(1)} async-done(((bf16[2,16,1,16,128]{4,1,2,0,3:T(8,128)(2,1)}), bf16[2,16,1,16,128]{4,1,2,0,3:T(8,128)(2,1)S(1)}, u32[]{:S(2)}, u32[]{:S(2)}) %all-to-all-start.2) | async-done | bytes 131104 | tf_op jit(solution)/shard_map/all_to_all | solution.py:85
  69.4 1.3 collective-permute-start.1
  70.7 5.1 %collective-permute-start = (bf16[2,16,32,1,128]{4,2,3,1,0:T(8,128)(2,1)S(1)}, bf16[2,16,32,1,128]{4,2,3,1,0:T(8,128)(2,1)S(1)}, u32[]{:S(2)}, u32[]{:S(2)}) collective-permute-start(bf16[2,16,32,1,128]{4,2,3,1,0:T(8,128)(2,1)S(1)} %pad_maximum_fusion), channel_id=1, source_target_pairs={{0,32},{32,64},{64,96},{96,128},{128,160},{160,192},{192,224},{224... | collective-permute-start | bytes 786440 | tf_op jit(solution)/shard_map/ppermute | solution.py:17
  75.8 0.7 fusion.145
  113.5 0.8 copy.114
  114.3 0.8 select_maximum_fusion
  115.1 1.8 %constant_dynamic-slice_fusion.20 = (bf16[2,16,32,1,128]{4,2,3,1,0:T(8,128)(2,1)S(1)}, bf16[2,16,32,1,128]{4,2,3,1,0:T(8,128)(2,1)S(1)}, bf16[2,16,32,1,128]{4,2...) fusion(bf16[2,16,32,3,132]{4,2,3,1,0:T(8,128)(2,1)S(1)} %select, ...), kind=kLoop, calls=%fused_computation.159 | loop fusion | bytes 8388668 | tf_op jit(solution)/shard_map/dynamic_slice | solution.py:62
  117.0 2.1 %constant_dynamic-slice_fusion = (bf16[2,16,32,1,128]{4,2,3,1,0:T(8,128)(2,1)S(1)}, bf16[2,16,32,1,128]{4,2,3,1,0:T(8,128)(2,1)S(1)}, bf16[2,16,32,1,128]{4,2,3,...) fusion(bf16[2,16,32,3,132]{4,2,3,1,0:T(8,128)(2,1)S(1)} %select, ...), kind=kLoop, calls=%fused_computation.139 | loop fusion | bytes 10485832 | tf_op jit(solution)/shard_map/dynamic_slice | solution.py:62
  120.7 0.4 fusion.77
  121.1 0.4 fusion.83
  121.5 0.4 fusion.89
  121.9 0.4 fusion.95
  122.4 0.4 fusion.101
  122.8 0.4 fusion.107
  123.2 6.1 %copy.157 = bf16[3,2,2,16,16,1,128]{4,3,0,6,1,2,5:T(8,128)(2,1)} copy(bf16[3,2,2,16,16,1,128]{6,4,2,3,1,0,5:T(8,128)(2,1)S(1)} %bitcast.450) | data formatting | bytes 1572864 | tf_op jit(solution)/shard_map/reshape | solution.py:69
  129.3 8.6 %copy.158 = bf16[2,16,16,2,384]{4,3,2,1,0:T(2,128)(2,1)} copy(bf16[2,16,16,2,384]{2,1,4,3,0:T(8,128)(2,1)} %bitcast.444) | data formatting | bytes 1572864 | tf_op jit(solution)/shard_map/reshape | solution.py:71
  (59 shorter events, 2.0 us)
Async XLA Ops:
  8.4 0.9 copy-start.4
  31.9 13.7 %copy-start = (bf16[2,6,16,6,32]{4,2,3,1,0:T(8,128)(2,1)S(1)}, bf16[2,6,16,6,32]{4,2,3,1,0:T(8,128)(2,1)}, u32[]{:S(2)}) copy-start(bf16[2,6,16,6,32]{4,2,3,1,0:T(8,128)(2,1)} %param.9) | copy-start | bytes 221188
  33.7 25.8 %copy-start.1 = (s32[6]{0:T(128)S(1)}, s32[6]{0:T(128)}, u32[]{:S(2)}) copy-start(s32[6]{0:T(128)} %param.8) | copy-start | bytes 76
  33.7 21.3 %all-to-all-start.1 = ((bf16[2,16,16,1,128]{4,1,3,0,2:T(8,128)(2,1)}), bf16[2,16,16,1,128]{4,1,3,0,2:T(8,128)(2,1)S(1)}, u32[]{:S(2)}, u32[]{:S(2)}) async-start(bf16[2,16,16,1,128]{4,1,3,0,2:T(8,128)(2,1)} %copy.115), calls=%async_computation.1 | async-start | bytes 262144 | tf_op jit(solution)/shard_map/all_to_all | solution.py:84
  56.0 13.3 %all-to-all-start.2 = ((bf16[2,16,1,16,128]{4,1,2,0,3:T(8,128)(2,1)}), bf16[2,16,1,16,128]{4,1,2,0,3:T(8,128)(2,1)S(1)}, u32[]{:S(2)}, u32[]{:S(2)}) async-start(bf16[2,16,1,16,128]{4,1,2,0,3:T(8,128)(2,1)} %copy.117), calls=%async_computation.2 | async-start | bytes 262144 | tf_op jit(solution)/shard_map/all_to_all | solution.py:85
  59.6 16.2 %copy-start.2 = (s32[6]{0:T(128)S(1)}, s32[6]{0:T(128)}, u32[]{:S(2)}) copy-start(s32[6]{0:T(128)} %param.7) | copy-start | bytes 76
  60.3 53.2 %copy-start.3 = (s32[1,128]{1,0:T(1,128)S(1)}, s32[1,128]{1,0:T(1,128)}, u32[]{:S(2)}) copy-start(s32[1,128]{1,0:T(1,128)} %param.6) | copy-start | bytes 1540
  69.4 45.0 %collective-permute-start.1 = (bf16[2,16,32,1,128]{4,2,3,1,0:T(8,128)(2,1)S(1)}, bf16[2,16,32,1,128]{4,2,3,1,0:T(8,128)(2,1)S(1)}, u32[]{:S(2)}, u32[]{:S(2)}) collective-permute-start(bf16[2,16,32,1,128]{4,2,3,1,0:T(8,128)(2,1)S(1)} %pad_maximum_fusion), channel_id=1, source_target_pairs={{32,0},{64,32},{96,64},{128,96},{160,128},{192,160},{224,192},{256... | collective-permute-start | bytes 786440 | tf_op jit(solution)/shard_map/ppermute | solution.py:19
  70.7 43.7 %collective-permute-start = (bf16[2,16,32,1,128]{4,2,3,1,0:T(8,128)(2,1)S(1)}, bf16[2,16,32,1,128]{4,2,3,1,0:T(8,128)(2,1)S(1)}, u32[]{:S(2)}, u32[]{:S(2)}) collective-permute-start(bf16[2,16,32,1,128]{4,2,3,1,0:T(8,128)(2,1)S(1)} %pad_maximum_fusion), channel_id=1, source_target_pairs={{0,32},{32,64},{64,96},{96,128},{128,160},{160,192},{192,224},{224... | collective-permute-start | bytes 786440 | tf_op jit(solution)/shard_map/ppermute | solution.py:17
where the time goes:
time: 141 us; the launch traced here: 138 us
  between operations  37.6 us (27%)
  local copies, waits for them, and re-layouts  29 us (21%)
  starting transfers between devices  21.7 us (15%)
  blocking collectives  19.6 us (14%)
  waiting for transfers between devices  17.6 us (12%)
  other arithmetic  9.53 us (7%)
  matrix products  2.94 us (2%)
    all_to_all x1, blocking collectives, local(): lax.all_to_all(spectra, 'gx', split_axis=1, concat_axis=4, tiled=True)  19.6 us
    all_to_all x1, starting transfers between devices, local(): lax.all_to_all(planes, 'kz', split_axis=2, concat_axis=3, tiled=True)  11.8 us
    all_to_all x1, waiting for transfers between devices, local(): lax.all_to_all(planes, 'kz', split_axis=2, concat_axis=3, tiled=True)  9.47 us
    reshape x1, local copies, waits for them, and re-layouts, fill_grid(): reordered.reshape(actual.shape[0], actual.shape[1], actual.shape[2], 2 *...  8.59 us
    another operation x2, other arithmetic  8.38 us
    all_to_all x1, waiting for transfers between devices, local(): lax.all_to_all(conjugate_flip(kz_slabs), 'kz', split_axis=3, concat_axis=...  8.11 us
    reshape x1, local copies, waits for them, and re-layouts, fill_grid(): stacked = jnp.stack(filled, axis=0).reshape((3, 2) + actual.shape)  6.07 us
    ppermute x1, starting transfers between devices, with_halo(): lax.ppermute(tail, axis, [(i, (i + 1) % count) for i in range(ends)])  5.08 us
  transfers between devices with their start and end apart: 4, of which 2 were waited for; matrix products, arithmetic and copies ran while one was open for 2% of the time, Pallas kernels for 0%

commit v1 on v0

v1 whole, which is shorter than its diff:
```python
import math

import jax
import jax.numpy as jnp
import numpy as np
from jax import lax
from jax.experimental import pallas as pl
from jax.experimental.pallas import tpu as pltpu
from jax.sharding import PartitionSpec as P

COILS = 16
NX = 512
NZC = 16
NY3 = 128
GX = 32
AL = NY3 // GX
NXL = NX // GX
SC = 2 * COILS
SHIFTS = 5
ROWS3 = 3
KDIM = ROWS3 * SHIFTS * 2 * SC
F32 = jnp.float32
BF16 = jnp.bfloat16


def dft_table():
    index = np.arange(NX)
    angle = (index[:, None] * index[None, :] % NX) * (2.0 * math.pi / NX)
    table = np.concatenate([np.cos(angle), np.sin(angle)], axis=1) / math.sqrt(NX)
    return jnp.asarray(table.astype(np.float32)).astype(BF16)


def iota(shape, dim):
    return lax.broadcasted_iota(jnp.int32, shape, dim)


def onehot(condition):
    return jnp.where(condition, 1.0, 0.0).astype(BF16)


def dot(a, b):
    return lax.dot_general(a, b, (((1,), (0,)), ((), ())), preferred_element_type=F32)


def dot_t(a, b):
    return lax.dot_general(a, b, (((1,), (1,)), ((), ())), preferred_element_type=F32)


def dft_kernel(lines_ref, table_ref, out_ref):
    lines = lines_ref[...].reshape(COILS * AL * 2, NX)
    size = COILS * AL * 2
    row, col = iota((size, size), 0), iota((size, size), 1)
    al, s, c = row // SC, (row // COILS) % 2, row % COILS
    line = (c * AL + al) * 2
    same = onehot(col == line + s)
    cross = onehot(col == line + 1 - s)
    cross = jnp.where(s == 0, -cross.astype(F32), cross.astype(F32)).astype(BF16)
    direct = dot(same, lines).astype(BF16)
    crossed = dot(cross, lines).astype(BF16)
    both = jnp.concatenate([direct, crossed], axis=1)
    spectra = dot_t(table_ref[...], both)
    out_ref[...] = spectra.astype(BF16).reshape(GX, NXL, size)


def dft(lines):
    return pl.pallas_call(
        dft_kernel,
        out_shape=jax.ShapeDtypeStruct((GX, NXL, COILS * AL * 2), BF16),
        name="dft",
    )(lines, dft_table())


def slab_kernel(in_ref, out_ref):
    value = in_ref[...].reshape(GX * NXL, AL * SC)
    size = GX * NXL
    row, col = iota((size, size), 0), iota((size, size), 1)
    order = onehot(col == (row % GX) * NXL + row // GX)
    rows = dot(order, value).astype(BF16)
    eye = onehot(iota((128, 128), 0) == iota((128, 128), 1))
    group = 128 // GX
    wide = AL * 128
    kk, nn = iota((wide, group * NY3), 0), iota((wide, group * NY3), 1)
    place = onehot(
        (kk % 128) // GX * NY3 + (kk % GX) * AL + kk // 128 == nn
    )
    for part in range(NXL // group):
        turned = dot_t(eye, rows[part * 128 : (part + 1) * 128]).astype(BF16)
        flat = jnp.concatenate(
            [turned[al * SC : (al + 1) * SC] for al in range(AL)], axis=1
        )
        spread = dot(flat, place).astype(BF16)
        for x in range(group):
            out_ref[part * group + x] = spread[:, x * NY3 : (x + 1) * NY3]


def to_slab(lines):
    return pl.pallas_call(
        slab_kernel,
        out_shape=jax.ShapeDtypeStruct((NXL, SC, NY3), BF16),
        name="slab",
    )(lines)


def fill_kernel(
    a0_ref, a1_ref, a2_ref, v0_ref, v1_ref, v2_ref, weight_ref, acquired_ref,
    out_ref, source_ref,
):
    lane_in = iota((NY3, SHIFTS * NY3), 0)
    lane_out = iota((NY3, SHIFTS * NY3), 1)
    want = lane_out % NY3 + lane_out // NY3 - 2
    straight = onehot(lane_in == want)
    mirrored = onehot(NY3 - 1 - lane_in == want)
    slabs = ((a0_ref, a1_ref, a2_ref, straight), (v0_ref, v1_ref, v2_ref, mirrored))
    for v in range(2):
        for rho in range(ROWS3):
            slab = slabs[v][rho][...].reshape(NXL * SC, NY3)
            moved = dot(slab, slabs[v][3]).astype(BF16)
            for d in range(SHIFTS):
                at = ((rho * SHIFTS + d) * 2 + v) * SC
                for x in range(NXL):
                    source_ref[x // 2, at : at + SC, (x % 2) * NY3 : (x % 2 + 1) * NY3] = moved[
                        x * SC : (x + 1) * SC, d * NY3 : (d + 1) * NY3
                    ]
    weights = weight_ref[...]
    acquired = acquired_ref[...]
    kk, nn = iota((3 * NY3, 3 * NY3), 0), iota((3 * NY3, 3 * NY3), 1)
    weave = onehot((kk % NY3) * 3 + kk // NY3 == nn)
    parity = iota((2 * SC, NY3), 0) % 2
    masks = [jnp.broadcast_to(acquired, (2 * SC, NY3)) == 2 * ry + parity for ry in range(3)]
    for pair in range(NXL // 2):
        result = dot(weights, source_ref[pair])
        for half in range(2):
            x = 2 * pair + half
            lanes = slice(half * NY3, (half + 1) * NY3)
            kept = result[6 * SC : 8 * SC, lanes]
            chosen = [
                jnp.where(masks[ry], kept, result[ry * 2 * SC : (ry + 1) * 2 * SC, lanes])
                for ry in range(3)
            ]
            line = jnp.concatenate(chosen, axis=1).astype(BF16)
            woven = dot(line, weave).astype(BF16)
            for s in range(2):
                out_ref[s, x] = woven[s * SC : (s + 1) * SC].reshape(COILS, 2, 3 * NY3)


def fill(slabs, weights, acquired_at):
    return pl.pallas_call(
        fill_kernel,
        out_shape=jax.ShapeDtypeStruct((2, NXL, COILS, 2, 3 * NY3), BF16),
        scratch_shapes=[pltpu.VMEM((NXL // 2, KDIM, 2 * NY3), BF16)],
        name="fill",
    )(*slabs, weights, acquired_at)


def placed_weights(kernels, ky_start, kz_start):
    real = kernels[0].reshape(6, COILS, 6, 2, COILS)
    imag = kernels[1].reshape(6, COILS, 6, 2, COILS)
    sign = jnp.asarray([1.0, -1.0], BF16)[:, None]
    to_real = jnp.stack([real, -imag * sign], axis=4)
    to_imag = jnp.stack([imag, real * sign], axis=4)
    parts = jnp.stack([to_real, to_imag], axis=1).reshape(6, 2, COILS, 6, 2 * SC)
    spot = jnp.arange(ROWS3 * SHIFTS, dtype=jnp.int32)
    placed = 0
    for j in range(2):
        for i in range(3):
            target = (kz_start + 1 + j) * SHIFTS + ky_start + 2 + i
            here = (target[:, None] == spot[None, :])[:, None, None, :, None]
            placed = placed + jnp.where(here, parts[:, :, :, 3 * j + i, None, :], jnp.zeros((), BF16))
    placed = placed.reshape(3, 2, 2, COILS, KDIM).transpose(0, 2, 3, 1, 4).reshape(6 * SC, KDIM)
    own = np.zeros((SC, 2, KDIM), np.float32)
    for sc in range(SC):
        own[sc, :, ((1 * SHIFTS + 2) * 2) * SC + sc] = 1.0
    own = jnp.asarray(own.reshape(2 * SC, KDIM)).astype(BF16)
    return jnp.concatenate([placed, own], axis=0)


def local(kspace_lines, acquired_at, ky_start, kz_start, kernels):
    spectra = dft(kspace_lines)
    gathered = lax.all_to_all(spectra, "gx", split_axis=0, concat_axis=0, tiled=True)
    own = to_slab(gathered)

    def fetch(offset_of):
        pairs = [(offset_of(b), b) for b in range(NZC) if 0 <= offset_of(b) < NZC]
        return lax.ppermute(own, "kz", pairs)

    below = fetch(lambda b: b - 1)
    above = fetch(lambda b: b + 1)
    mirror = fetch(lambda b: NZC - 1 - b)
    mirror_below = fetch(lambda b: NZC - b)
    mirror_above = fetch(lambda b: NZC - 2 - b)
    weights = placed_weights(kernels, ky_start, kz_start)
    return fill(
        (below, own, above, mirror_below, mirror, mirror_above), weights, acquired_at
    )


def solution(mesh):
    placed = (P(None, "kz", "gx", None, None), P("kz", None), P(), P(), P())
    return jax.shard_map(
        local,
        mesh=mesh,
        in_specs=placed,
        out_specs=P(None, "gx", None, "kz", None),
        check_vma=False,
    )
```

time: 141 us -> 73.6 us (0.52); the launches traced: 138 us -> 73.2 us
  between operations: 37.6 us -> 0.47 us
  local copies, waits for them, and re-layouts: 29 us -> 8.39 us
  blocking collectives: 19.6 us -> 0 us
  starting transfers between devices: 21.7 us -> 40.2 us
  Pallas kernels: 0 us -> 13.3 us
  waiting for transfers between devices: 17.6 us -> 4.92 us
  other arithmetic: 9.53 us -> 6.01 us
  matrix products: 2.94 us -> 0 us
    ppermute x2 -> x5, starting transfers between devices: 6.37 us -> 29.6 us  [fetch(): return lax.ppermute(own, 'kz', pairs)]
    all_to_all x1 -> x0, blocking collectives: 19.6 us -> none  [local(): lax.all_to_all(spectra, 'gx', split_axis=1, concat_axis=4, tiled=True)]
    all_to_all x2 -> x1, waiting for transfers between devices: 17.6 us -> 0.01 us  [local(): lax.all_to_all(spectra, 'gx', split_axis=0, concat_axis=0, tiled=True)]
    reshape x2 -> x1, local copies, waits for them, and re-layouts: 14.7 us -> 0.28 us  [placed_weights(): placed.reshape(3, 2, 2, COILS, KDIM).transpose(0, 2, 3, 1, 4)]
    pallas_call x0 -> x3, Pallas kernels: none -> 13.3 us  [the longest x1 7.81 us: fill(): pl.pallas_call(fill_kernel, out_shape=jax.ShapeDtypeStruct((2, NXL, COILS...]
    another operation x4 -> x1, other arithmetic: 8.66 us -> 3.15 us  [placed_weights(): to_real = jnp.stack([real, -imag * sign], axis=4)]
    ppermute x2 -> x5, waiting for transfers between devices: 0.01 us -> 4.92 us  [fetch(): return lax.ppermute(own, 'kz', pairs)]
    all_to_all x2 -> x1, starting transfers between devices: 15.3 us -> 10.6 us  [local(): lax.all_to_all(spectra, 'gx', split_axis=0, concat_axis=0, tiled=True)]
  transfers between devices with their start and end apart: 4 -> 6, of which waited for: 2 -> 1; matrix products, arithmetic and copies ran while one was open for 2% -> 17% of each run, Pallas kernels for 0% -> 0%
where the time goes in v1:
time: 73.6 us; the launch traced here: 73.2 us
  starting transfers between devices  40.2 us (55%)
  Pallas kernels  13.3 us (18%)
  local copies, waits for them, and re-layouts  8.39 us (11%)
  other arithmetic  6.01 us (8%)
  waiting for transfers between devices  4.92 us (7%)
    ppermute x5, starting transfers between devices, fetch(): return lax.ppermute(own, 'kz', pairs)  29.6 us
    all_to_all x1, starting transfers between devices, local(): lax.all_to_all(spectra, 'gx', split_axis=0, concat_axis=0, tiled=True)  10.6 us
    pallas_call x1, Pallas kernels, fill(): pl.pallas_call(fill_kernel, out_shape=jax.ShapeDtypeStruct((2, NXL, COILS...  7.81 us
    ppermute x5, waiting for transfers between devices, fetch(): return lax.ppermute(own, 'kz', pairs)  4.92 us
    broadcast_in_dim x24, local copies, waits for them, and re-layouts, placed_weights(): jnp.where(here, parts[:, :, :, 3 * j + i, None, :], jnp.zeros((), BF16))  4.6 us
    another operation x1, other arithmetic, placed_weights(): to_real = jnp.stack([real, -imag * sign], axis=4)  3.15 us
    pallas_call x1, Pallas kernels, to_slab(): pl.pallas_call(slab_kernel, out_shape=jax.ShapeDtypeStruct((NXL, SC, NY3)...  2.87 us
    pallas_call x1, Pallas kernels, dft(): pl.pallas_call(dft_kernel, out_shape=jax.ShapeDtypeStruct((GX, NXL, COILS...  2.6 us
  transfers between devices with their start and end apart: 6, of which 1 were waited for; matrix products, arithmetic and copies ran while one was open for 17% of the time, Pallas kernels for 0%

profile of v1, /device:TPU:1, one launch (start us, length us, event | category | flops | bytes accessed | tf_op | source)
XLA Modules:
  0.0 73.2 jit_solution(9539581378318954232)
XLA Ops:
  0.0 2.6 %dft.1 = bf16[32,16,128]{2,1,0:T(8,128)(2,1)} custom-call(bf16[16,1,4,2,512]{4,3,2,1,0:T(2,128)(2,1)} %lines_ref.1, bf16[512,1024]{1,0:T(8,128)(2,1)} %constant.26.table_ref), custom_call_target="tpu_custom_call" | custom-call | tf_op jit(solution)/shard_map/dft/pallas_call | solution.py:66
  2.6 10.6 %all-to-all-start = ((bf16[32,16,128]{2,1,0:T(8,128)(2,1)}), bf16[32,16,128]{2,1,0:T(8,128)(2,1)S(1)}, u32[]{:S(2)}, u32[]{:S(2)}) async-start(bf16[32,16,128]{2,1,0:T(8,128)(2,1)} %dft.1), calls=%async_computation | async-start | bytes 262144 | tf_op jit(solution)/shard_map/all_to_all | solution.py:179
  13.2 0.3 reshape_squeeze.5
  13.5 0.3 stack_reshape_squeeze.5
  13.8 1.3 %broadcast_multiply_fusion = (bf16[6,16,6,2,1,16]{5,4,3,1,2,0:T(2,128)(2,1)S(1)}, bf16[6,16,6,2,1,16]{5,4,3,1,2,0:T(2,128)(2,1)S(1)}) fusion(bf16[6,16,6,2,1,16]{5,4,3,1,2,0:T(2,128)(2,1)S(1)} %stack_reshape_squeeze.5, bf16[2]{0:T(256)(128)(2,1)S(1)} %copy-done.8, bf16[6,16,6,2,1,16]{5,4,3,1,2,0:T(2,128)(2,1)S(1)} %reshape_squeeze.5), kind=kLoop, calls=%fused_computation.5 | loop fusion | flops 55296 | bytes 147460 | tf_op jit(solution)/shard_map/mul | solution.py:160
  15.2 3.1 %pad_maximum_fusion = (bf16[6,16,6,2,2,16]{5,4,3,1,2,0:T(2,128)(2,1)S(1)}, bf16[6,16,6,2,2,16]{5,4,3,1,2,0:T(2,128)(2,1)S(1)}) fusion(bf16[6,16,6,2,1,16]{5,4,3,1,2,0:T(2,128)(2,1)S(1)} %get-tuple-element.24, bf16[6,16,6,2,1,16]{5,4,3,1,2,0:T(2,128)(2,1)S(1)} %stack_reshape_squeeze.5, bf16[6,16,6,2,1,16]{5,4,3,1,2,0:T(2,128)(2,1)S(1)} %get-tuple-element.23, ...), kind=kLoop, calls=%fused_computation | loop fusion | flops 294912 | bytes 294912 | tf_op jit(solution)/shard_map/stack | solution.py:159
  18.3 0.3 stack.18
  18.7 0.3 stack.20
  19.0 0.2 copy-done.9
  19.6 0.1 broadcast_in_dim.145
  19.7 0.5 broadcast_in_dim.146
  20.2 0.1 broadcast_in_dim.152
  20.4 0.5 broadcast_in_dim.153
  21.0 0.5 broadcast_in_dim.159
  21.6 0.5 broadcast_in_dim.165
  22.2 0.5 broadcast_in_dim.171
  22.9 0.5 broadcast_in_dim.177
  24.5 0.6 copy-done
  25.2 2.9 %slab.1.a1_ref = bf16[16,32,128]{2,1,0:T(8,128)(2,1)} custom-call(bf16[32,16,128]{2,1,0:T(8,128)(2,1)} %copy-done), custom_call_target="tpu_custom_call" | custom-call | tf_op jit(solution)/shard_map/slab/pallas_call | solution.py:97
  28.1 5.8 %collective-permute-start = (bf16[16,32,128]{2,1,0:T(8,128)(2,1)}, bf16[16,32,128]{2,1,0:T(8,128)(2,1)S(1)}, u32[]{:S(2)}, u32[]{:S(2)}) collective-permute-start(bf16[16,32,128]{2,1,0:T(8,128)(2,1)} %slab.1.a1_ref), channel_id=1, source_target_pairs={{0,32},{32,64},{64,96},{96,128},{128,160},{160,192},{192,224},{224... | collective-permute-start | bytes 393224 | tf_op jit(solution)/shard_map/ppermute | solution.py:184
  33.9 1.3 %collective-permute-start.1 = (bf16[16,32,128]{2,1,0:T(8,128)(2,1)}, bf16[16,32,128]{2,1,0:T(8,128)(2,1)S(1)}, u32[]{:S(2)}, u32[]{:S(2)}) collective-permute-start(bf16[16,32,128]{2,1,0:T(8,128)(2,1)} %slab.1.a1_ref), channel_id=1, source_target_pairs={{32,0},{64,32},{96,64},{128,96},{160,128},{192,160},{224,192},{256... | collective-permute-start | bytes 393224 | tf_op jit(solution)/shard_map/ppermute | solution.py:184
  35.2 0.7 collective-permute-start.2
  35.8 13.4 %collective-permute-start.3 = (bf16[16,32,128]{2,1,0:T(8,128)(2,1)}, bf16[16,32,128]{2,1,0:T(8,128)(2,1)S(1)}, u32[]{:S(2)}, u32[]{:S(2)}) collective-permute-start(bf16[16,32,128]{2,1,0:T(8,128)(2,1)} %slab.1.a1_ref), channel_id=1, source_target_pairs={{480,0},{448,32},{416,64},{384,96},{352,128},{320,160},{288,192},{... | collective-permute-start | bytes 393224 | tf_op jit(solution)/shard_map/ppermute | solution.py:184
  49.2 8.5 %collective-permute-start.4 = (bf16[16,32,128]{2,1,0:T(8,128)(2,1)}, bf16[16,32,128]{2,1,0:T(8,128)(2,1)S(1)}, u32[]{:S(2)}, u32[]{:S(2)}) collective-permute-start(bf16[16,32,128]{2,1,0:T(8,128)(2,1)} %slab.1.a1_ref), channel_id=1, source_target_pairs={{448,0},{416,32},{384,64},{352,96},{320,128},{288,160},{256,192},{... | collective-permute-start | bytes 393224 | tf_op jit(solution)/shard_map/ppermute | solution.py:184
  57.7 0.3 add_bitcast_fusion
  58.0 0.4 copy.19
  58.4 0.3 reshape.165
  58.7 0.2 copy-done.7
  58.9 0.8 %pad_maximum_fusion.2.weight_ref = bf16[256,960]{1,0:T(8,128)(2,1)} fusion(bf16[64,960]{1,0:T(8,128)(2,1)S(1)} %copy-done.7, bf16[192,960]{1,0:T(8,128)(2,1)S(1)} %reshape.165), kind=kLoop, calls=%fused_computation.3 | loop fusion | flops 983040 | bytes 983040 | tf_op jit(solution)/shard_map/concatenate | solution.py:174
  59.8 4.9 %collective-permute-done.4.v2_ref = bf16[16,32,128]{2,1,0:T(8,128)(2,1)S(1)} collective-permute-done((bf16[16,32,128]{2,1,0:T(8,128)(2,1)}, bf16[16,32,128]{2,1,0:T(8,128)(2,1)S(1)}, u32[]{:S(2)}, u32[]{:S(2)}) %collective-permute-start.4) | collective-permute-done | bytes 131104 | tf_op jit(solution)/shard_map/ppermute | solution.py:184
  64.8 0.6 copy-done.6
  65.4 7.8 %fill.1 = bf16[2,16,16,2,384]{4,3,2,1,0:T(2,128)(2,1)} custom-call(bf16[16,32,128]{2,1,0:T(8,128)(2,1)} %copy-done.2, bf16[16,32,128]{2,1,0:T(8,128)(2,1)} %slab.1.a1_ref, bf16[16,32,128]{2,1,0:T(8,128)(2,1)} %copy-done.3, bf16[16,32,128]{2,1,0:T(8,128)(2,1)} %copy-done.4, bf16[16,32,128]{2,1,0:T(8,128)(2,1)} %copy-done.5, bf16[16,32,128]{2,1,0:T(8,128)(2,1)} %copy-done.6, ...), custom_call_target="tpu_custom_call" | custom-call | tf_op jit(solution)/shard_map/fill/pallas_call | solution.py:147
  (56 shorter events, 2.1 us)
Async XLA Ops:
  0.0 13.2 %copy-start.1 = (bf16[2,6,16,6,32]{4,2,3,1,0:T(8,128)(2,1)S(1)}, bf16[2,6,16,6,32]{4,2,3,1,0:T(8,128)(2,1)}, u32[]{:S(2)}) copy-start(bf16[2,6,16,6,32]{4,2,3,1,0:T(8,128)(2,1)} %param.12) | copy-start | bytes 221188
  2.6 21.9 %all-to-all-start = ((bf16[32,16,128]{2,1,0:T(8,128)(2,1)}), bf16[32,16,128]{2,1,0:T(8,128)(2,1)S(1)}, u32[]{:S(2)}, u32[]{:S(2)}) async-start(bf16[32,16,128]{2,1,0:T(8,128)(2,1)} %dft.1), calls=%async_computation | async-start | bytes 262144 | tf_op jit(solution)/shard_map/all_to_all | solution.py:179
  13.2 0.7 copy-start.8
  18.6 0.7 copy-start.9
  18.6 0.7 copy-start.10
  24.5 0.7 copy-start
  28.1 31.7 %collective-permute-start = (bf16[16,32,128]{2,1,0:T(8,128)(2,1)}, bf16[16,32,128]{2,1,0:T(8,128)(2,1)S(1)}, u32[]{:S(2)}, u32[]{:S(2)}) collective-permute-start(bf16[16,32,128]{2,1,0:T(8,128)(2,1)} %slab.1.a1_ref), channel_id=1, source_target_pairs={{0,32},{32,64},{64,96},{96,128},{128,160},{160,192},{192,224},{224... | collective-permute-start | bytes 393224 | tf_op jit(solution)/shard_map/ppermute | solution.py:184
  33.9 25.9 %collective-permute-start.1 = (bf16[16,32,128]{2,1,0:T(8,128)(2,1)}, bf16[16,32,128]{2,1,0:T(8,128)(2,1)S(1)}, u32[]{:S(2)}, u32[]{:S(2)}) collective-permute-start(bf16[16,32,128]{2,1,0:T(8,128)(2,1)} %slab.1.a1_ref), channel_id=1, source_target_pairs={{32,0},{64,32},{96,64},{128,96},{160,128},{192,160},{224,192},{256... | collective-permute-start | bytes 393224 | tf_op jit(solution)/shard_map/ppermute | solution.py:184
  35.2 24.6 %collective-permute-start.2 = (bf16[16,32,128]{2,1,0:T(8,128)(2,1)}, bf16[16,32,128]{2,1,0:T(8,128)(2,1)S(1)}, u32[]{:S(2)}, u32[]{:S(2)}) collective-permute-start(bf16[16,32,128]{2,1,0:T(8,128)(2,1)} %slab.1.a1_ref), channel_id=1, source_target_pairs={{480,32},{448,64},{416,96},{384,128},{352,160},{320,192},{288,224}... | collective-permute-start | bytes 393224 | tf_op jit(solution)/shard_map/ppermute | solution.py:184
  35.8 24.0 %collective-permute-start.3 = (bf16[16,32,128]{2,1,0:T(8,128)(2,1)}, bf16[16,32,128]{2,1,0:T(8,128)(2,1)S(1)}, u32[]{:S(2)}, u32[]{:S(2)}) collective-permute-start(bf16[16,32,128]{2,1,0:T(8,128)(2,1)} %slab.1.a1_ref), channel_id=1, source_target_pairs={{480,0},{448,32},{416,64},{384,96},{352,128},{320,160},{288,192},{... | collective-permute-start | bytes 393224 | tf_op jit(solution)/shard_map/ppermute | solution.py:184
  49.2 15.5 %collective-permute-start.4 = (bf16[16,32,128]{2,1,0:T(8,128)(2,1)}, bf16[16,32,128]{2,1,0:T(8,128)(2,1)S(1)}, u32[]{:S(2)}, u32[]{:S(2)}) collective-permute-start(bf16[16,32,128]{2,1,0:T(8,128)(2,1)} %slab.1.a1_ref), channel_id=1, source_target_pairs={{448,0},{416,32},{384,64},{352,96},{320,128},{288,160},{256,192},{... | collective-permute-start | bytes 393224 | tf_op jit(solution)/shard_map/ppermute | solution.py:184
  58.0 0.9 %copy-start.7 = (bf16[64,960]{1,0:T(8,128)(2,1)S(1)}, bf16[64,960]{1,0:T(8,128)(2,1)}, u32[]{:S(2)}) copy-start(bf16[64,960]{1,0:T(8,128)(2,1)} %constant.27) | copy-start | bytes 368644
  59.8 5.0 %copy-start.2 = (bf16[16,32,128]{2,1,0:T(8,128)(2,1)}, bf16[16,32,128]{2,1,0:T(8,128)(2,1)S(1)}, u32[]{:S(2)}) copy-start(bf16[16,32,128]{2,1,0:T(8,128)(2,1)S(1)} %collective-permute-done.a0_ref) | copy-start | bytes 393220
  59.8 5.0 %copy-start.3 = (bf16[16,32,128]{2,1,0:T(8,128)(2,1)}, bf16[16,32,128]{2,1,0:T(8,128)(2,1)S(1)}, u32[]{:S(2)}) copy-start(bf16[16,32,128]{2,1,0:T(8,128)(2,1)S(1)} %collective-permute-done.1.a2_ref) | copy-start | bytes 393220
  59.8 5.0 %copy-start.4 = (bf16[16,32,128]{2,1,0:T(8,128)(2,1)}, bf16[16,32,128]{2,1,0:T(8,128)(2,1)S(1)}, u32[]{:S(2)}) copy-start(bf16[16,32,128]{2,1,0:T(8,128)(2,1)S(1)} %collective-permute-done.2.v0_ref) | copy-start | bytes 393220
  59.8 4.9 %copy-start.5 = (bf16[16,32,128]{2,1,0:T(8,128)(2,1)}, bf16[16,32,128]{2,1,0:T(8,128)(2,1)S(1)}, u32[]{:S(2)}) copy-start(bf16[16,32,128]{2,1,0:T(8,128)(2,1)S(1)} %collective-permute-done.3.v1_ref) | copy-start | bytes 393220
  64.8 0.6 copy-start.6

commit v2 on v1

v2 whole, which is shorter than its diff:
```python
import math

import jax
import jax.numpy as jnp
import numpy as np
from jax import lax
from jax.experimental import pallas as pl
from jax.experimental.pallas import tpu as pltpu
from jax.sharding import PartitionSpec as P

COILS = 16
NX = 512
NZC = 16
NY3 = 128
GX = 32
AL = NY3 // GX
NXL = NX // GX
SC = 2 * COILS
SHIFTS = 5
ROWS3 = 3
KDIM = ROWS3 * SHIFTS * 2 * SC
KPAD = 1024
F32 = jnp.float32
BF16 = jnp.bfloat16


def dft_table():
    index = np.arange(NX // 2)
    angle = (index[:, None] * index[None, :] % NX) * (2.0 * math.pi / NX)
    table = np.concatenate([np.cos(angle), np.sin(angle)], axis=1) / math.sqrt(NX)
    return jnp.asarray(table.astype(np.float32)).astype(BF16)


def iota(shape, dim):
    return lax.broadcasted_iota(jnp.int32, shape, dim)


def onehot(condition):
    return jnp.where(condition, 1.0, 0.0).astype(BF16)


def dot(a, b):
    return lax.dot_general(a, b, (((1,), (0,)), ((), ())), preferred_element_type=F32)


def dot_t(a, b):
    return lax.dot_general(a, b, (((1,), (1,)), ((), ())), preferred_element_type=F32)


def room(mib):
    return pltpu.CompilerParams(vmem_limit_bytes=mib << 20)


def column_onehot(target, lanes):
    return onehot(target == iota((target.shape[0], lanes), 1))


def dft_kernel(lines_hbm, table_hbm, out_ref, lines_ref, table_ref, sems):
    lines_copy = pltpu.make_async_copy(lines_hbm, lines_ref, sems.at[0])
    table_copy = pltpu.make_async_copy(table_hbm, table_ref, sems.at[1])
    lines_copy.start()
    table_copy.start()
    size = COILS * AL * 2
    row = iota((size, 1), 0)
    al, s, c = row // SC, (row // COILS) % 2, row % COILS
    line = (c * AL + al) * 2
    same = column_onehot(line + s, size)
    cross = column_onehot(line + 1 - s, size).astype(F32)
    cross = jnp.where(s == 0, -cross, cross).astype(BF16)
    lines_copy.wait()
    lines = lines_ref[...].reshape(size, NX)
    direct = dot(same, lines)
    crossed = dot(cross, lines)
    half = NX // 2
    flip = iota((size, half), 1) % 2 == 0
    parts = [
        jnp.concatenate([direct[:, lanes], crossed[:, lanes]], axis=1)
        for lanes in (slice(0, half), slice(half, NX))
    ]
    flip = iota((size, NX), 1) % 2 == 0
    parts += [jnp.where(flip, part, -part) for part in parts]
    stacked = jnp.concatenate(parts, axis=0).astype(BF16)
    table_copy.wait()
    sums = dot_t(table_ref[...], stacked)
    even = iota((half, size), 0) % 2 == 0
    for upper in range(2):
        first = sums[:, 2 * upper * size : (2 * upper + 1) * size]
        second = sums[:, (2 * upper + 1) * size : (2 * upper + 2) * size]
        spectra = (first + jnp.where(even, second, -second)).astype(BF16)
        out_ref[upper * GX // 2 : (upper + 1) * GX // 2] = spectra.reshape(GX // 2, NXL, size)


def dft(lines):
    hbm = pl.BlockSpec(memory_space=pltpu.HBM)
    return pl.pallas_call(
        dft_kernel,
        out_shape=jax.ShapeDtypeStruct((GX, NXL, COILS * AL * 2), BF16),
        in_specs=[hbm, hbm],
        scratch_shapes=[
            pltpu.VMEM((COILS, 1, AL, 2, NX), BF16),
            pltpu.VMEM((NX // 2, NX), BF16),
            pltpu.SemaphoreType.DMA((2,)),
        ],
        compiler_params=room(62),
        name="dft",
    )(lines, dft_table())


def slab_kernel(in_ref, out_ref, rows_ref):
    rows_ref[...] = in_ref[...].reshape(GX * NXL, AL * SC).astype(F32)
    eye = column_onehot(iota((128, 1), 0), 128)
    group = 128 // GX
    k = iota((AL * 128, 1), 0)
    place = column_onehot((k % 128) // GX * NY3 + (k % GX) * AL + k // 128, group * NY3)
    flats = []
    for part in range(NXL // group):
        rows = jnp.concatenate(
            [rows_ref[pl.ds(part * group + x, GX, stride=NXL), :] for x in range(group)], axis=0
        ).astype(BF16)
        turned = dot_t(eye, rows).astype(BF16)
        flats.append(
            jnp.concatenate([turned[al * SC : (al + 1) * SC] for al in range(AL)], axis=1)
        )
    spread = dot(jnp.concatenate(flats, axis=0), place).astype(BF16)
    for part in range(NXL // group):
        for x in range(group):
            out_ref[part * group + x] = spread[
                part * SC : (part + 1) * SC, x * NY3 : (x + 1) * NY3
            ]


def to_slab(lines):
    return pl.pallas_call(
        slab_kernel,
        out_shape=jax.ShapeDtypeStruct((NXL, SC, NY3), BF16),
        scratch_shapes=[pltpu.VMEM((GX * NXL, AL * SC), F32)],
        compiler_params=room(8),
        name="slab",
    )(lines)


def weights_kernel(ky_ref, kz_ref, kernels_ref, out_ref, wide_ref, placed_ref):
    direct, crossed = [], []
    for t in range(6):
        for p in range(6):
            real, imag = kernels_ref[0, t, p], kernels_ref[1, t, p]
            direct += [real, imag]
            crossed += [(-imag.astype(F32)).astype(BF16), real]
    direct = jnp.concatenate(direct, axis=0)
    crossed = jnp.concatenate(crossed, axis=0)
    h = iota((2 * COILS, 1), 0)
    v, coil = h // COILS, h % COILS
    for odd in range(2):
        at = odd * 2 * SC + v * SC + coil
        plain = column_onehot(at, 4 * SC)
        swapped = column_onehot(at + COILS, 4 * SC).astype(F32)
        swapped = jnp.where(v == 0, swapped, -swapped).astype(BF16)
        wide = (dot(direct, plain) + dot(crossed, swapped)).astype(BF16)
        wide_ref[odd] = wide.reshape(36, SC, 4 * SC)
    b = lax.axis_index("kz")
    zero = jnp.zeros((SC, 4 * SC), BF16)
    for t in range(6):
        kz, ky = kz_ref[t], ky_ref[t]
        for pair in range(8):
            total = None
            for odd in range(2):
                q = 2 * pair + odd
                if q >= ROWS3 * SHIFTS:
                    continue
                row, shift = q // SHIFTS - 1, q % SHIFTS - 2
                j, i = row - kz, shift - ky
                used = (j >= 0) & (j < 2) & (i >= 0) & (i < 3)
                if row == -1:
                    used = used & (b > 0)
                if row == 1:
                    used = used & (b < NZC - 1)
                p = jnp.where(used, 3 * j + i, 0)
                block = jnp.where(used, wide_ref[odd, t * 6 + p], zero)
                total = block if total is None else total + block
            placed_ref[t // 2, (t % 2) * SC : (t % 2 + 1) * SC, pair * 4 * SC : (pair + 1) * 4 * SC] = total
    r = iota((2 * SC, 1), 0)
    weave = column_onehot((r % 2) * SC + r // 2, 2 * SC)
    for ry in range(3):
        out_ref[ry * 2 * SC : (ry + 1) * 2 * SC] = dot(weave, placed_ref[ry]).astype(BF16)
    out_ref[6 * SC :] = column_onehot((SHIFTS + 2) * 2 * SC + r // 2, KPAD)


def placed_weights(kernels, ky_start, kz_start):
    smem = pl.BlockSpec(memory_space=pltpu.SMEM)
    vmem = pl.BlockSpec(memory_space=pltpu.VMEM)
    return pl.pallas_call(
        weights_kernel,
        out_shape=jax.ShapeDtypeStruct((8 * SC, KPAD), BF16),
        in_specs=[smem, smem, vmem],
        scratch_shapes=[
            pltpu.VMEM((2, 36, SC, 4 * SC), BF16),
            pltpu.VMEM((3, 2 * SC, KPAD), BF16),
        ],
        cost_estimate=pl.CostEstimate(flops=100_000_000, bytes_accessed=4_000_000, transcendentals=0),
        compiler_params=room(12),
        name="weights",
    )(ky_start, kz_start, kernels.transpose(0, 1, 3, 2, 4))


def fill_kernel(
    own_ref, next0_ref, next1_ref, mirror_ref, near_ref, far_ref, weight_ref,
    acquired_ref, out_ref, source_ref,
):
    odd = lax.axis_index("kz") % 2
    k = iota((NY3, 1), 0)
    lane = iota((NY3, SHIFTS * NY3), 1)
    want = lane % NY3 + lane // NY3 - 2
    straight = onehot(k == want)
    mirrored = onehot(NY3 - 1 - k == want)

    def spread(slab, moves, v, row, first):
        count = slab.shape[0]
        moved = dot(slab.reshape(count * SC, NY3), moves).astype(BF16)
        for d in range(SHIFTS):
            at = ((row * SHIFTS + d) * 2 + v) * SC
            if not isinstance(row, int):
                at = pl.multiple_of(at, SC)
            for n in range(count):
                x = first + n
                source_ref[x // 2, pl.ds(at, SC), (x % 2) * NY3 : (x % 2 + 1) * NY3] = moved[
                    n * SC : (n + 1) * SC, d * NY3 : (d + 1) * NY3
                ]

    spread(own_ref[...], straight, 0, 1, 0)
    spread(next0_ref[...], straight, 0, 2 - 2 * odd, 0)
    spread(next1_ref[...], straight, 0, 2 * odd, 0)
    spread(mirror_ref[...], mirrored, 1, 1, 0)
    spread(near_ref[...], mirrored, 1, 2 * odd, 0)
    spread(far_ref[...], mirrored, 1, 2 - 2 * odd, 0)
    weights = weight_ref[:, :KDIM]
    acquired = acquired_ref[...]
    n = iota((3 * NY3, 1), 0)
    weave = column_onehot((n % NY3) * 3 + n // NY3, 3 * NY3)
    parity = iota((2 * SC, NY3), 0) % 2
    masks = [jnp.broadcast_to(acquired, (2 * SC, NY3)) == 2 * ry + parity for ry in range(3)]
    for pair in range(NXL // 2):
        result = dot(weights, source_ref[pair])
        for half in range(2):
            x = 2 * pair + half
            lanes = slice(half * NY3, (half + 1) * NY3)
            kept = result[6 * SC : 8 * SC, lanes]
            chosen = [
                jnp.where(masks[ry], kept, result[ry * 2 * SC : (ry + 1) * 2 * SC, lanes])
                for ry in range(3)
            ]
            line = jnp.concatenate(chosen, axis=1).astype(BF16)
            woven = dot(line, weave).astype(BF16)
            for s in range(2):
                out_ref[s, x] = woven[s * SC : (s + 1) * SC].reshape(COILS, 2, 3 * NY3)


def fill(slabs, weights, acquired_at):
    return pl.pallas_call(
        fill_kernel,
        out_shape=jax.ShapeDtypeStruct((2, NXL, COILS, 2, 3 * NY3), BF16),
        scratch_shapes=[pltpu.VMEM((NXL // 2, KDIM, 2 * NY3), BF16)],
        compiler_params=room(24),
        name="fill",
    )(*slabs, weights, acquired_at)


def local(kspace_lines, acquired_at, ky_start, kz_start, kernels):
    spectra = dft(kspace_lines)
    gathered = lax.all_to_all(spectra, "gx", split_axis=0, concat_axis=0, tiled=True)
    weights = placed_weights(kernels, ky_start, kz_start)
    own = to_slab(gathered)

    def fetch(values, source_of):
        pairs = [(source_of(b) % NZC, b) for b in range(NZC)]
        return lax.ppermute(values, "kz", pairs)

    next1 = fetch(own, lambda b: b - 1 + 2 * (b % 2))
    next0 = fetch(own, lambda b: b + 1 - 2 * (b % 2))
    near = fetch(own, lambda b: NZC - 2 * (b % 2) - b)
    mirror = fetch(own, lambda b: NZC - 1 - b)
    far = fetch(next1, lambda b: NZC - 3 + 4 * (b % 2) - b)
    return fill((own, next0, next1, mirror, near, far), weights, acquired_at)


def solution(mesh):
    placed = (P(None, "kz", "gx", None, None), P("kz", None), P(), P(), P())
    return jax.shard_map(
        local,
        mesh=mesh,
        in_specs=placed,
        out_specs=P(None, "gx", None, "kz", None),
        check_vma=False,
    )
```

time: 73.6 us -> 64 us (0.87)
  starting transfers between devices: 40.2 us -> 20.1 us
  blocking collectives: 0 us -> 19.9 us
  local copies, waits for them, and re-layouts: 8.39 us -> 0.03 us
  waiting for transfers between devices: 4.92 us -> 12.8 us
  other arithmetic: 6.01 us -> 0 us
  Pallas kernels: 13.3 us -> 10.6 us
    all_to_all x0 -> x1, blocking collectives: none -> 19.9 us  [local(): lax.all_to_all(spectra, 'gx', split_axis=0, concat_axis=0, tiled=True)]
    all_to_all x1 -> x0, starting transfers between devices: 10.6 us -> none  [local(): lax.all_to_all(spectra, 'gx', split_axis=0, concat_axis=0, tiled=True)]
    ppermute x5, starting transfers between devices: 29.6 us -> 20.1 us  [fetch(): return lax.ppermute(values, 'kz', pairs)]
    ppermute x5, waiting for transfers between devices: 4.92 us -> 12.8 us  [fetch(): return lax.ppermute(values, 'kz', pairs)]
    broadcast_in_dim x24 -> x0, local copies, waits for them, and re-layouts: 4.6 us -> none  [placed_weights(): jnp.where(here, parts[:, :, :, 3 * j + i, None, :], jnp.zeros((), BF16))]
    another operation x1 -> x0, other arithmetic: 3.15 us -> none  [placed_weights(): to_real = jnp.stack([real, -imag * sign], axis=4)]
    pallas_call x1, Pallas kernels: 2.87 us -> 0.43 us  [to_slab(): pl.pallas_call(slab_kernel, out_shape=jax.ShapeDtypeStruct((NXL, SC, NY3)...]
    unnamed x23 -> x8, local copies, waits for them, and re-layouts: 1.83 us -> 0.03 us
  transfers between devices with their start and end apart: 6 -> 5, of which waited for: 1 -> 3; matrix products, arithmetic and copies ran while one was open for 17% -> 0% of each run, Pallas kernels for 0% -> 2%
where the time goes in v2:
time: 64 us; the launch traced here: 63.7 us
  starting transfers between devices  20.1 us (31%)
  blocking collectives  19.9 us (31%)
  waiting for transfers between devices  12.8 us (20%)
  Pallas kernels  10.6 us (17%)
    ppermute x5, starting transfers between devices, fetch(): return lax.ppermute(values, 'kz', pairs)  20.1 us
    all_to_all x1, blocking collectives, local(): lax.all_to_all(spectra, 'gx', split_axis=0, concat_axis=0, tiled=True)  19.9 us
    ppermute x5, waiting for transfers between devices, fetch(): return lax.ppermute(values, 'kz', pairs)  12.8 us
    pallas_call x1, Pallas kernels, fill(): pl.pallas_call(fill_kernel, out_shape=jax.ShapeDtypeStruct((2, NXL, COILS...  6.56 us
    pallas_call x1, Pallas kernels, dft(): pl.pallas_call(dft_kernel, out_shape=jax.ShapeDtypeStruct((GX, NXL, COILS...  2.13 us
    pallas_call x1, Pallas kernels, placed_weights(): pl.pallas_call(weights_kernel, out_shape=jax.ShapeDtypeStruct((8 * SC, KP...  1.5 us
  transfers between devices with their start and end apart: 5, of which 3 were waited for; matrix products, arithmetic and copies ran while one was open for 0% of the time, Pallas kernels for 2%

profile of v2, /device:TPU:1, one launch (start us, length us, event | category | flops | bytes accessed | tf_op | source)
XLA Modules:
  0.0 63.7 jit_solution(12560103491575715126)
XLA Ops:
  0.0 2.1 %dft.1 = bf16[32,16,128]{2,1,0:T(8,128)(2,1)} custom-call(bf16[16,1,4,2,512]{4,3,2,1,0:T(2,128)(2,1)} %lines_hbm.1, bf16[256,512]{1,0:T(8,128)(2,1)} %constant.5.table_hbm), custom_call_target="tpu_custom_call" | custom-call | tf_op jit(solution)/shard_map/dft/pallas_call | solution.py:95
  2.1 0.0 copy-start
  2.1 19.9 %all_to_all.5.in_ref = bf16[32,16,128]{2,1,0:T(8,128)(2,1)S(1)} all-to-all(bf16[32,16,128]{2,1,0:T(8,128)(2,1)} %dft.1), channel_id=1, replica_groups=mesh['kz'=16,'gx'=32] {'gx'}, dimensions={0} | all-to-all | bytes 262144 | tf_op jit(solution)/shard_map/all_to_all | solution.py:269
  22.1 0.4 slab.1.own_ref
  22.5 0.0 copy-start.1
  22.5 0.0 copy-start.2
  22.5 11.9 %collective-permute-start.1 = (bf16[16,32,128]{2,1,0:T(8,128)(2,1)S(1)}, bf16[16,32,128]{2,1,0:T(8,128)(2,1)S(1)}, u32[]{:S(2)}, u32[]{:S(2)}) collective-permute-start(bf16[16,32,128]{2,1,0:T(8,128)(2,1)S(1)} %slab.1.own_ref), channel_id=1, source_target_pairs={{480,0},{64,32},{32,64},{128,96},{96,128},{192,160},{160,192},{256... | collective-permute-start | bytes 393224 | tf_op jit(solution)/shard_map/ppermute | solution.py:275
  34.5 0.7 %collective-permute-start.3 = (bf16[16,32,128]{2,1,0:T(8,128)(2,1)S(1)}, bf16[16,32,128]{2,1,0:T(8,128)(2,1)S(1)}, u32[]{:S(2)}, u32[]{:S(2)}) collective-permute-start(bf16[16,32,128]{2,1,0:T(8,128)(2,1)S(1)} %slab.1.own_ref), channel_id=1, source_target_pairs={{0,0},{416,32},{448,64},{352,96},{384,128},{288,160},{320,192},{22... | collective-permute-start | bytes 393224 | tf_op jit(solution)/shard_map/ppermute | solution.py:275
  35.2 1.9 %collective-permute-start.2 = (bf16[16,32,128]{2,1,0:T(8,128)(2,1)S(1)}, bf16[16,32,128]{2,1,0:T(8,128)(2,1)S(1)}, u32[]{:S(2)}, u32[]{:S(2)}) collective-permute-start(bf16[16,32,128]{2,1,0:T(8,128)(2,1)S(1)} %slab.1.own_ref), channel_id=1, source_target_pairs={{480,0},{448,32},{416,64},{384,96},{352,128},{320,160},{288,192},{... | collective-permute-start | bytes 393224 | tf_op jit(solution)/shard_map/ppermute | solution.py:275
  37.1 3.7 %collective-permute-start = (bf16[16,32,128]{2,1,0:T(8,128)(2,1)S(1)}, bf16[16,32,128]{2,1,0:T(8,128)(2,1)S(1)}, u32[]{:S(2)}, u32[]{:S(2)}) collective-permute-start(bf16[16,32,128]{2,1,0:T(8,128)(2,1)S(1)} %slab.1.own_ref), channel_id=1, source_target_pairs={{32,0},{0,32},{96,64},{64,96},{160,128},{128,160},{224,192},{192,2... | collective-permute-start | bytes 393224 | tf_op jit(solution)/shard_map/ppermute | solution.py:275
  40.8 2.2 %collective-permute-done.1.next1_ref = bf16[16,32,128]{2,1,0:T(8,128)(2,1)S(1)} collective-permute-done((bf16[16,32,128]{2,1,0:T(8,128)(2,1)S(1)}, bf16[16,32,128]{2,1,0:T(8,128)(2,1)S(1)}, u32[]{:S(2)}, u32[]{:S(2)}) %collective-permute-start.1) | collective-permute-done | bytes 131104 | tf_op jit(solution)/shard_map/ppermute | solution.py:275
  43.1 1.9 %collective-permute-start.4 = (bf16[16,32,128]{2,1,0:T(8,128)(2,1)S(1)}, bf16[16,32,128]{2,1,0:T(8,128)(2,1)S(1)}, u32[]{:S(2)}, u32[]{:S(2)}) collective-permute-start(bf16[16,32,128]{2,1,0:T(8,128)(2,1)S(1)} %collective-permute-done.1.next1_ref), channel_id=1, source_target_pairs={{416,0},{0,32},{352,64},{448,96},{288,128},{384,160},{224,192},{32... | collective-permute-start | bytes 393224 | tf_op jit(solution)/shard_map/ppermute | solution.py:275
  45.0 0.0 copy-done
  45.0 0.0 copy-done.1
  45.0 0.0 copy-done.2
  45.0 0.0 copy-start.3
  45.0 1.5 %weights.1.weight_ref = bf16[256,1024]{1,0:T(8,128)(2,1)S(1)} custom-call(s32[6]{0:T(128)S(1)} %copy-done.1, s32[6]{0:T(128)S(1)} %copy-done.2, bf16[2,6,6,16,32]{4,3,2,1,0:T(8,128)(2,1)S(1)} %bitcast.1), custom_call_target="tpu_custom_call" | custom-call | flops 100000000 | bytes 4000000 | tf_op jit(solution)/shard_map/weights/pallas_call | solution.py:191
  46.5 0.0 collective-permute-done.3.near_ref
  46.5 0.0 collective-permute-done.2.mirror_ref
  46.5 1.1 %collective-permute-done.next0_ref = bf16[16,32,128]{2,1,0:T(8,128)(2,1)S(1)} collective-permute-done((bf16[16,32,128]{2,1,0:T(8,128)(2,1)S(1)}, bf16[16,32,128]{2,1,0:T(8,128)(2,1)S(1)}, u32[]{:S(2)}, u32[]{:S(2)}) %collective-permute-start) | collective-permute-done | bytes 131104 | tf_op jit(solution)/shard_map/ppermute | solution.py:275
  47.6 9.5 %collective-permute-done.4.far_ref = bf16[16,32,128]{2,1,0:T(8,128)(2,1)S(1)} collective-permute-done((bf16[16,32,128]{2,1,0:T(8,128)(2,1)S(1)}, bf16[16,32,128]{2,1,0:T(8,128)(2,1)S(1)}, u32[]{:S(2)}, u32[]{:S(2)}) %collective-permute-start.4) | collective-permute-done | bytes 131104 | tf_op jit(solution)/shard_map/ppermute | solution.py:275
  57.1 0.0 copy-done.3
  57.1 6.6 %fill.1 = bf16[2,16,16,2,384]{4,3,2,1,0:T(2,128)(2,1)} custom-call(bf16[16,32,128]{2,1,0:T(8,128)(2,1)S(1)} %slab.1.own_ref, bf16[16,32,128]{2,1,0:T(8,128)(2,1)S(1)} %collective-permute-done.next0_ref, bf16[16,32,128]{2,1,0:T(8,128)(2,1)S(1)} %collective-permute-done.1.next1_ref, bf16[16,32,128]{2,1,0:T(8,128)(2,1)S(1)} %collective-permute-done.2.mirror_ref, ...), custom_call_target="tpu_custom_call" | custom-call | tf_op jit(solution)/shard_map/fill/pallas_call | solution.py:258
Async XLA Ops:
  2.1 42.8 %copy-start = (bf16[2,6,16,6,32]{4,2,3,1,0:T(8,128)(2,1)S(1)}, bf16[2,6,16,6,32]{4,2,3,1,0:T(8,128)(2,1)}, u32[]{:S(2)}) copy-start(bf16[2,6,16,6,32]{4,2,3,1,0:T(8,128)(2,1)} %param.10) | copy-start | bytes 221188
  22.5 22.5 %copy-start.1 = (s32[6]{0:T(128)S(1)}, s32[6]{0:T(128)}, u32[]{:S(2)}) copy-start(s32[6]{0:T(128)} %ky_ref.1) | copy-start | bytes 76
  22.5 22.5 %copy-start.2 = (s32[6]{0:T(128)S(1)}, s32[6]{0:T(128)}, u32[]{:S(2)}) copy-start(s32[6]{0:T(128)} %kz_ref.1) | copy-start | bytes 76
  22.5 20.5 %collective-permute-start.1 = (bf16[16,32,128]{2,1,0:T(8,128)(2,1)S(1)}, bf16[16,32,128]{2,1,0:T(8,128)(2,1)S(1)}, u32[]{:S(2)}, u32[]{:S(2)}) collective-permute-start(bf16[16,32,128]{2,1,0:T(8,128)(2,1)S(1)} %slab.1.own_ref), channel_id=1, source_target_pairs={{480,0},{64,32},{32,64},{128,96},{96,128},{192,160},{160,192},{256... | collective-permute-start | bytes 393224 | tf_op jit(solution)/shard_map/ppermute | solution.py:275
  34.5 12.0 %collective-permute-start.3 = (bf16[16,32,128]{2,1,0:T(8,128)(2,1)S(1)}, bf16[16,32,128]{2,1,0:T(8,128)(2,1)S(1)}, u32[]{:S(2)}, u32[]{:S(2)}) collective-permute-start(bf16[16,32,128]{2,1,0:T(8,128)(2,1)S(1)} %slab.1.own_ref), channel_id=1, source_target_pairs={{0,0},{416,32},{448,64},{352,96},{384,128},{288,160},{320,192},{22... | collective-permute-start | bytes 393224 | tf_op jit(solution)/shard_map/ppermute | solution.py:275
  35.2 11.4 %collective-permute-start.2 = (bf16[16,32,128]{2,1,0:T(8,128)(2,1)S(1)}, bf16[16,32,128]{2,1,0:T(8,128)(2,1)S(1)}, u32[]{:S(2)}, u32[]{:S(2)}) collective-permute-start(bf16[16,32,128]{2,1,0:T(8,128)(2,1)S(1)} %slab.1.own_ref), channel_id=1, source_target_pairs={{480,0},{448,32},{416,64},{384,96},{352,128},{320,160},{288,192},{... | collective-permute-start | bytes 393224 | tf_op jit(solution)/shard_map/ppermute | solution.py:275
  37.1 10.5 %collective-permute-start = (bf16[16,32,128]{2,1,0:T(8,128)(2,1)S(1)}, bf16[16,32,128]{2,1,0:T(8,128)(2,1)S(1)}, u32[]{:S(2)}, u32[]{:S(2)}) collective-permute-start(bf16[16,32,128]{2,1,0:T(8,128)(2,1)S(1)} %slab.1.own_ref), channel_id=1, source_target_pairs={{32,0},{0,32},{96,64},{64,96},{160,128},{128,160},{224,192},{192,2... | collective-permute-start | bytes 393224 | tf_op jit(solution)/shard_map/ppermute | solution.py:275
  43.1 14.1 %collective-permute-start.4 = (bf16[16,32,128]{2,1,0:T(8,128)(2,1)S(1)}, bf16[16,32,128]{2,1,0:T(8,128)(2,1)S(1)}, u32[]{:S(2)}, u32[]{:S(2)}) collective-permute-start(bf16[16,32,128]{2,1,0:T(8,128)(2,1)S(1)} %collective-permute-done.1.next1_ref), channel_id=1, source_target_pairs={{416,0},{0,32},{352,64},{448,96},{288,128},{384,160},{224,192},{32... | collective-permute-start | bytes 393224 | tf_op jit(solution)/shard_map/ppermute | solution.py:275
  45.0 12.1 %copy-start.3 = (s32[1,128]{1,0:T(1,128)S(1)}, s32[1,128]{1,0:T(1,128)}, u32[]{:S(2)}) copy-start(s32[1,128]{1,0:T(1,128)} %acquired_ref.1) | copy-start | bytes 1540

commit v3 on v2

--- a/solution.py
+++ b/solution.py
@@ -7,6 +7,7 @@
 from jax.experimental import pallas as pl
 from jax.experimental.pallas import tpu as pltpu
 from jax.sharding import PartitionSpec as P
+
 
 COILS = 16
 NX = 512
@@ -20,6 +21,8 @@
 ROWS3 = 3
 KDIM = ROWS3 * SHIFTS * 2 * SC
 KPAD = 1024
+KFAR = SHIFTS * SC
+FARPAD = 384
 F32 = jnp.float32
 BF16 = jnp.bfloat16
 
@@ -139,7 +142,9 @@
     )(lines)
 
 
-def weights_kernel(ky_ref, kz_ref, kernels_ref, out_ref, wide_ref, placed_ref):
+def weights_kernel(
+    ky_ref, kz_ref, kernels_ref, out_ref, far_ref, wide_ref, placed_ref, placed_far_ref
+):
     direct, crossed = [], []
     for t in range(6):
         for p in range(6):
@@ -159,29 +164,37 @@
         wide_ref[odd] = wide.reshape(36, SC, 4 * SC)
     b = lax.axis_index("kz")
     zero = jnp.zeros((SC, 4 * SC), BF16)
+
+    def block(t, odd, row, shift):
+        j, i = row - kz_ref[t], shift - 2 - ky_ref[t]
+        used = (j >= 0) & (j < 2) & (i >= 0) & (i < 3) & (b + row >= 0) & (b + row < NZC)
+        return jnp.where(used, wide_ref[odd, t * 6 + jnp.where(used, 3 * j + i, 0)], zero)
+
+    far_row = 1 - 2 * (b % 2)
     for t in range(6):
-        kz, ky = kz_ref[t], ky_ref[t]
+        rows = slice((t % 2) * SC, (t % 2 + 1) * SC)
         for pair in range(8):
-            total = None
-            for odd in range(2):
-                q = 2 * pair + odd
-                if q >= ROWS3 * SHIFTS:
-                    continue
-                row, shift = q // SHIFTS - 1, q % SHIFTS - 2
-                j, i = row - kz, shift - ky
-                used = (j >= 0) & (j < 2) & (i >= 0) & (i < 3)
-                if row == -1:
-                    used = used & (b > 0)
-                if row == 1:
-                    used = used & (b < NZC - 1)
-                p = jnp.where(used, 3 * j + i, 0)
-                block = jnp.where(used, wide_ref[odd, t * 6 + p], zero)
-                total = block if total is None else total + block
-            placed_ref[t // 2, (t % 2) * SC : (t % 2 + 1) * SC, pair * 4 * SC : (pair + 1) * 4 * SC] = total
+            lanes = slice(pair * 4 * SC, (pair + 1) * 4 * SC)
+            total = block(t, 0, pair * 2 // SHIFTS - 1, pair * 2 % SHIFTS)
+            if pair < 7:
+                q = pair * 2 + 1
+                total = total + block(t, 1, q // SHIFTS - 1, q % SHIFTS)
+            placed_ref[t // 2, rows, lanes] = total
+        for pair in range(3):
+            lanes = slice(pair * 4 * SC, (pair + 1) * 4 * SC)
+            total = block(t, 0, far_row, pair * 2)
+            if pair < 2:
+                total = total + block(t, 1, far_row, pair * 2 + 1)
+            placed_far_ref[t // 2, rows, lanes] = total
     r = iota((2 * SC, 1), 0)
     weave = column_onehot((r % 2) * SC + r // 2, 2 * SC)
+    k, lane = iota((FARPAD, 1), 0), iota((FARPAD, KFAR), 1)
+    virtual = onehot(k == lane // SC * 2 * SC + SC + lane % SC)
     for ry in range(3):
-        out_ref[ry * 2 * SC : (ry + 1) * 2 * SC] = dot(weave, placed_ref[ry]).astype(BF16)
+        rows = slice(ry * 2 * SC, (ry + 1) * 2 * SC)
+        out_ref[rows] = dot(weave, placed_ref[ry]).astype(BF16)
+        far = dot(weave, placed_far_ref[ry]).astype(BF16)
+        far_ref[rows] = dot(far, virtual).astype(BF16)
     out_ref[6 * SC :] = column_onehot((SHIFTS + 2) * 2 * SC + r // 2, KPAD)
 
 
@@ -190,11 +203,15 @@
     vmem = pl.BlockSpec(memory_space=pltpu.VMEM)
     return pl.pallas_call(
         weights_kernel,
-        out_shape=jax.ShapeDtypeStruct((8 * SC, KPAD), BF16),
+        out_shape=(
+            jax.ShapeDtypeStruct((8 * SC, KPAD), BF16),
+            jax.ShapeDtypeStruct((6 * SC, KFAR), BF16),
+        ),
         in_specs=[smem, smem, vmem],
         scratch_shapes=[
             pltpu.VMEM((2, 36, SC, 4 * SC), BF16),
             pltpu.VMEM((3, 2 * SC, KPAD), BF16),
+            pltpu.VMEM((3, 2 * SC, FARPAD), BF16),
         ],
         cost_estimate=pl.CostEstimate(flops=100_000_000, bytes_accessed=4_000_000, transcendentals=0),
         compiler_params=room(12),
@@ -202,72 +219,112 @@
     )(ky_start, kz_start, kernels.transpose(0, 1, 3, 2, 4))
 
 
-def fill_kernel(
-    own_ref, next0_ref, next1_ref, mirror_ref, near_ref, far_ref, weight_ref,
-    acquired_ref, out_ref, source_ref,
-):
-    odd = lax.axis_index("kz") % 2
+def spread(source_ref, slab, mirrored, at_of):
     k = iota((NY3, 1), 0)
     lane = iota((NY3, SHIFTS * NY3), 1)
     want = lane % NY3 + lane // NY3 - 2
-    straight = onehot(k == want)
-    mirrored = onehot(NY3 - 1 - k == want)
-
-    def spread(slab, moves, v, row, first):
-        count = slab.shape[0]
-        moved = dot(slab.reshape(count * SC, NY3), moves).astype(BF16)
-        for d in range(SHIFTS):
-            at = ((row * SHIFTS + d) * 2 + v) * SC
-            if not isinstance(row, int):
-                at = pl.multiple_of(at, SC)
-            for n in range(count):
-                x = first + n
-                source_ref[x // 2, pl.ds(at, SC), (x % 2) * NY3 : (x % 2 + 1) * NY3] = moved[
-                    n * SC : (n + 1) * SC, d * NY3 : (d + 1) * NY3
-                ]
-
-    spread(own_ref[...], straight, 0, 1, 0)
-    spread(next0_ref[...], straight, 0, 2 - 2 * odd, 0)
-    spread(next1_ref[...], straight, 0, 2 * odd, 0)
-    spread(mirror_ref[...], mirrored, 1, 1, 0)
-    spread(near_ref[...], mirrored, 1, 2 * odd, 0)
-    spread(far_ref[...], mirrored, 1, 2 - 2 * odd, 0)
+    moves = onehot((NY3 - 1 - k if mirrored else k) == want)
+    moved = dot(slab.reshape(NXL * SC, NY3), moves).astype(BF16)
+    for d in range(SHIFTS):
+        for x in range(NXL):
+            source_ref[x // 2, pl.ds(at_of(d), SC), (x % 2) * NY3 : (x % 2 + 1) * NY3] = moved[
+                x * SC : (x + 1) * SC, d * NY3 : (d + 1) * NY3
+            ]
+
+
+def early_kernel(
+    own_ref, next0_ref, next1_ref, mirror_ref, near_ref, weight_ref, sums_ref, source_ref
+):
+    odd = lax.axis_index("kz") % 2
+
+    def at(row, v):
+        return lambda d: pl.multiple_of(((row * SHIFTS + d) * 2 + v) * SC, SC)
+
+    first, last = 2 * odd, 2 - 2 * odd
+    for d in range(SHIFTS):
+        for pair in range(NXL // 2):
+            source_ref[pair, pl.ds(at(last, 1)(d), SC), :] = jnp.zeros((SC, 2 * NY3), BF16)
+    spread(source_ref, own_ref[...], False, at(1, 0))
+    spread(source_ref, next1_ref[...], False, at(first, 0))
+    spread(source_ref, near_ref[...], True, at(first, 1))
+    spread(source_ref, mirror_ref[...], True, at(1, 1))
+    spread(source_ref, next0_ref[...], False, at(last, 0))
     weights = weight_ref[:, :KDIM]
+    for pair in range(NXL // 2):
+        sums_ref[pair] = dot(weights, source_ref[pair])
+
+
+def early(slabs, weights):
+    return pl.pallas_call(
+        early_kernel,
+        out_shape=jax.ShapeDtypeStruct((NXL // 2, 8 * SC, 2 * NY3), F32),
+        scratch_shapes=[pltpu.VMEM((NXL // 2, KDIM, 2 * NY3), BF16)],
+        compiler_params=room(16),
+        cost_estimate=pl.CostEstimate(
+            flops=1_500_000_000, bytes_accessed=4_000_000, transcendentals=0
+        ),
+        name="early",
+    )(*slabs, weights)
+
+
+def late_kernel(
+    sums_ref, far_ref, weight_ref, acquired_ref, out_hbm, source_ref, out_ref, sems
+):
+    spread(source_ref, far_ref[...], True, lambda d: d * SC)
+    weights = weight_ref[...]
     acquired = acquired_ref[...]
     n = iota((3 * NY3, 1), 0)
     weave = column_onehot((n % NY3) * 3 + n // NY3, 3 * NY3)
     parity = iota((2 * SC, NY3), 0) % 2
     masks = [jnp.broadcast_to(acquired, (2 * SC, NY3)) == 2 * ry + parity for ry in range(3)]
+    copies = []
     for pair in range(NXL // 2):
-        result = dot(weights, source_ref[pair])
+        result = dot(weights, source_ref[pair]) + sums_ref[pair, : 6 * SC]
+        lines = []
         for half in range(2):
-            x = 2 * pair + half
             lanes = slice(half * NY3, (half + 1) * NY3)
-            kept = result[6 * SC : 8 * SC, lanes]
+            kept = sums_ref[pair, 6 * SC :, lanes]
             chosen = [
                 jnp.where(masks[ry], kept, result[ry * 2 * SC : (ry + 1) * 2 * SC, lanes])
                 for ry in range(3)
             ]
-            line = jnp.concatenate(chosen, axis=1).astype(BF16)
-            woven = dot(line, weave).astype(BF16)
+            lines.append(jnp.concatenate(chosen, axis=1).astype(BF16))
+        woven = dot(jnp.concatenate(lines, axis=0), weave).astype(BF16)
+        for half in range(2):
             for s in range(2):
-                out_ref[s, x] = woven[s * SC : (s + 1) * SC].reshape(COILS, 2, 3 * NY3)
-
-
-def fill(slabs, weights, acquired_at):
-    return pl.pallas_call(
-        fill_kernel,
-        out_shape=jax.ShapeDtypeStruct((2, NXL, COILS, 2, 3 * NY3), BF16),
-        scratch_shapes=[pltpu.VMEM((NXL // 2, KDIM, 2 * NY3), BF16)],
-        compiler_params=room(24),
-        name="fill",
-    )(*slabs, weights, acquired_at)
+                at = (half * 2 + s) * SC
+                out_ref[s, 2 * pair + half] = woven[at : at + SC].reshape(COILS, 2, 3 * NY3)
+        for s in range(2):
+            two = pl.ds(2 * pair, 2)
+            copy = pltpu.make_async_copy(out_ref.at[s, two], out_hbm.at[s, two], sems.at[s, pair])
+            copy.start()
+            copies.append(copy)
+    for copy in copies:
+        copy.wait()
+
+
+def late(sums, far, weights, acquired_at):
+    vmem = pl.BlockSpec(memory_space=pltpu.VMEM)
+    shape = (2, NXL, COILS, 2, 3 * NY3)
+    return pl.pallas_call(
+        late_kernel,
+        out_shape=jax.ShapeDtypeStruct(shape, BF16),
+        in_specs=[vmem] * 4,
+        out_specs=pl.BlockSpec(memory_space=pltpu.HBM),
+        scratch_shapes=[
+            pltpu.VMEM((NXL // 2, KFAR, 2 * NY3), BF16),
+            pltpu.VMEM(shape, BF16),
+            pltpu.SemaphoreType.DMA((2, NXL // 2)),
+        ],
+        compiler_params=room(16),
+        name="late",
+    )(sums, far, weights, acquired_at)
 
 
 def local(kspace_lines, acquired_at, ky_start, kz_start, kernels):
     spectra = dft(kspace_lines)
     gathered = lax.all_to_all(spectra, "gx", split_axis=0, concat_axis=0, tiled=True)
-    weights = placed_weights(kernels, ky_start, kz_start)
+    weights, far_weights = placed_weights(kernels, ky_start, kz_start)
     own = to_slab(gathered)
 
     def fetch(values, source_of):
@@ -279,7 +336,8 @@
     near = fetch(own, lambda b: NZC - 2 * (b % 2) - b)
     mirror = fetch(own, lambda b: NZC - 1 - b)
     far = fetch(next1, lambda b: NZC - 3 + 4 * (b % 2) - b)
-    return fill((own, next0, next1, mirror, near, far), weights, acquired_at)
+    sums = early((own, next0, next1, mirror, near), weights)
+    return late(sums, far, far_weights, acquired_at)
 
 
 def solution(mesh):

time: 64 us -> 60.7 us (0.948)
  waiting for transfers between devices: 12.8 us -> 5.72 us
  starting transfers between devices: 20.1 us -> 22.5 us
  local copies, waits for them, and re-layouts: 0.03 us -> 2.27 us
  Pallas kernels: 10.6 us -> 9.94 us
    ppermute x5, waiting for transfers between devices: 12.8 us -> 5.72 us  [fetch(): return lax.ppermute(values, 'kz', pairs)]
    ppermute x5, starting transfers between devices: 20.1 us -> 22.5 us  [fetch(): return lax.ppermute(values, 'kz', pairs)]
    unnamed x8, local copies, waits for them, and re-layouts: 0.03 us -> 2.27 us
    pallas_call x2 -> x3, Pallas kernels: 8.07 us -> 7.38 us  [the longest x1 2.96 us: late(): pl.pallas_call(late_kernel, out_shape=jax.ShapeDtypeStruct(shape, BF16),...]
  transfers between devices with their start and end apart: 5 -> 5, of which waited for: 3 -> 1; matrix products, arithmetic and copies ran while one was open for 0% -> 0% of each run, Pallas kernels for 2% -> 7%
where the time goes in v3:
time: 60.7 us; the launch traced here: 60.4 us
  starting transfers between devices  22.5 us (37%)
  blocking collectives  19.8 us (33%)
  Pallas kernels  9.94 us (16%)
  waiting for transfers between devices  5.72 us (9%)
  local copies, waits for them, and re-layouts  2.27 us (4%)
    ppermute x5, starting transfers between devices, fetch(): return lax.ppermute(values, 'kz', pairs)  22.5 us
    all_to_all x1, blocking collectives, local(): lax.all_to_all(spectra, 'gx', split_axis=0, concat_axis=0, tiled=True)  19.8 us
    ppermute x5, waiting for transfers between devices, fetch(): return lax.ppermute(values, 'kz', pairs)  5.72 us
    pallas_call x1, Pallas kernels, late(): pl.pallas_call(late_kernel, out_shape=jax.ShapeDtypeStruct(shape, BF16),...  2.96 us
    pallas_call x1, Pallas kernels, early(): pl.pallas_call(early_kernel, out_shape=jax.ShapeDtypeStruct((NXL // 2, 8...  2.39 us
    unnamed x8, local copies, waits for them, and re-layouts  2.27 us
    pallas_call x1, Pallas kernels, dft(): pl.pallas_call(dft_kernel, out_shape=jax.ShapeDtypeStruct((GX, NXL, COILS...  2.13 us
    pallas_call x1, Pallas kernels, placed_weights(): pl.pallas_call(weights_kernel, out_shape=(jax.ShapeDtypeStruct((8 * SC, K...  2.03 us
  transfers between devices with their start and end apart: 5, of which 1 were waited for; matrix products, arithmetic and copies ran while one was open for 0% of the time, Pallas kernels for 7%

profile of v3, /device:TPU:1, one launch (start us, length us, event | category | flops | bytes accessed | tf_op | source)
XLA Modules:
  0.0 60.4 jit_solution(2448079529872988577)
XLA Ops:
  0.0 2.1 %dft.1 = bf16[32,16,128]{2,1,0:T(8,128)(2,1)} custom-call(bf16[16,1,4,2,512]{4,3,2,1,0:T(2,128)(2,1)} %lines_hbm.1, bf16[256,512]{1,0:T(8,128)(2,1)} %constant.5.table_hbm), custom_call_target="tpu_custom_call" | custom-call | tf_op jit(solution)/shard_map/dft/pallas_call | solution.py:98
  2.1 19.8 %all_to_all.5.in_ref = bf16[32,16,128]{2,1,0:T(8,128)(2,1)S(1)} all-to-all(bf16[32,16,128]{2,1,0:T(8,128)(2,1)} %dft.1), channel_id=1, replica_groups=mesh['kz'=16,'gx'=32] {'gx'}, dimensions={0} | all-to-all | bytes 262144 | tf_op jit(solution)/shard_map/all_to_all | solution.py:326
  21.9 0.4 slab.1.own_ref
  22.4 11.9 %collective-permute-start.1 = (bf16[16,32,128]{2,1,0:T(8,128)(2,1)S(1)}, bf16[16,32,128]{2,1,0:T(8,128)(2,1)S(1)}, u32[]{:S(2)}, u32[]{:S(2)}) collective-permute-start(bf16[16,32,128]{2,1,0:T(8,128)(2,1)S(1)} %slab.1.own_ref), channel_id=1, source_target_pairs={{480,0},{64,32},{32,64},{128,96},{96,128},{192,160},{160,192},{256... | collective-permute-start | bytes 393224 | tf_op jit(solution)/shard_map/ppermute | solution.py:332
  34.3 1.9 %collective-permute-start = (bf16[16,32,128]{2,1,0:T(8,128)(2,1)S(1)}, bf16[16,32,128]{2,1,0:T(8,128)(2,1)S(1)}, u32[]{:S(2)}, u32[]{:S(2)}) collective-permute-start(bf16[16,32,128]{2,1,0:T(8,128)(2,1)S(1)} %slab.1.own_ref), channel_id=1, source_target_pairs={{32,0},{0,32},{96,64},{64,96},{160,128},{128,160},{224,192},{192,2... | collective-permute-start | bytes 393224 | tf_op jit(solution)/shard_map/ppermute | solution.py:332
  36.3 2.2 %collective-permute-start.2 = (bf16[16,32,128]{2,1,0:T(8,128)(2,1)S(1)}, bf16[16,32,128]{2,1,0:T(8,128)(2,1)S(1)}, u32[]{:S(2)}, u32[]{:S(2)}) collective-permute-start(bf16[16,32,128]{2,1,0:T(8,128)(2,1)S(1)} %slab.1.own_ref), channel_id=1, source_target_pairs={{480,0},{448,32},{416,64},{384,96},{352,128},{320,160},{288,192},{... | collective-permute-start | bytes 393224 | tf_op jit(solution)/shard_map/ppermute | solution.py:332
  38.4 0.7 %collective-permute-start.3 = (bf16[16,32,128]{2,1,0:T(8,128)(2,1)S(1)}, bf16[16,32,128]{2,1,0:T(8,128)(2,1)S(1)}, u32[]{:S(2)}, u32[]{:S(2)}) collective-permute-start(bf16[16,32,128]{2,1,0:T(8,128)(2,1)S(1)} %slab.1.own_ref), channel_id=1, source_target_pairs={{0,0},{416,32},{448,64},{352,96},{384,128},{288,160},{320,192},{22... | collective-permute-start | bytes 393224 | tf_op jit(solution)/shard_map/ppermute | solution.py:332
  39.1 0.0 copy-start.1
  39.1 1.0 %copy-done.1 = bf16[2,6,16,6,32]{4,2,3,1,0:T(8,128)(2,1)S(1)} copy-done((bf16[2,6,16,6,32]{4,2,3,1,0:T(8,128)(2,1)S(1)}, bf16[2,6,16,6,32]{4,2,3,1,0:T(8,128)(2,1)}, u32[]{:S(2)}) %copy-start.1) | copy-done | bytes 73752
  40.1 0.0 copy-start.2
  40.1 0.7 %copy-done.2 = s32[6]{0:T(128)S(1)} copy-done((s32[6]{0:T(128)S(1)}, s32[6]{0:T(128)}, u32[]{:S(2)}) %copy-start.2) | copy-done | bytes 48
  40.7 0.0 copy-start.3
  40.7 0.7 %copy-done.3 = s32[6]{0:T(128)S(1)} copy-done((s32[6]{0:T(128)S(1)}, s32[6]{0:T(128)}, u32[]{:S(2)}) %copy-start.3) | copy-done | bytes 48
  41.4 2.0 %weights.1 = (bf16[256,1024]{1,0:T(8,128)(2,1)S(1)}, bf16[192,160]{1,0:T(8,128)(2,1)S(1)}) custom-call(s32[6]{0:T(128)S(1)} %copy-done.2, s32[6]{0:T(128)S(1)} %copy-done.3, bf16[2,6,6,16,32]{4,3,2,1,0:T(8,128)(2,1)S(1)} %bitcast.1), custom_call_target="tpu_custom_call" | custom-call | flops 100000000 | bytes 4000000 | tf_op jit(solution)/shard_map/weights/pallas_call | solution.py:204
  43.4 0.0 collective-permute-done.1.next1_ref
  43.4 5.8 %collective-permute-start.4 = (bf16[16,32,128]{2,1,0:T(8,128)(2,1)S(1)}, bf16[16,32,128]{2,1,0:T(8,128)(2,1)S(1)}, u32[]{:S(2)}, u32[]{:S(2)}) collective-permute-start(bf16[16,32,128]{2,1,0:T(8,128)(2,1)S(1)} %collective-permute-done.1.next1_ref), channel_id=1, source_target_pairs={{416,0},{0,32},{352,64},{448,96},{288,128},{384,160},{224,192},{32... | collective-permute-start | bytes 393224 | tf_op jit(solution)/shard_map/ppermute | solution.py:332
  49.2 0.0 collective-permute-done.next0_ref
  49.3 0.0 collective-permute-done.2.mirror_ref
  49.3 0.0 collective-permute-done.3.near_ref
  49.3 0.0 copy-start
  49.3 2.4 %early.1.sums_ref = f32[8,256,256]{2,1,0:T(8,128)S(1)} custom-call(bf16[16,32,128]{2,1,0:T(8,128)(2,1)S(1)} %slab.1.own_ref, bf16[16,32,128]{2,1,0:T(8,128)(2,1)S(1)} %collective-permute-done.next0_ref, bf16[16,32,128]{2,1,0:T(8,128)(2,1)S(1)} %collective-permute-done.1.next1_ref, bf16[16,32,128]{2,1,0:T(8,128)(2,1)S(1)} %collective-permute-done.2.mirror_ref, ...), custom_call_target="tpu_custom_call" | custom-call | flops 1500000000 | bytes 4000000 | tf_op jit(solution)/shard_map/early/pallas_call | solution.py:258
  51.7 5.7 %collective-permute-done.4.far_ref = bf16[16,32,128]{2,1,0:T(8,128)(2,1)S(1)} collective-permute-done((bf16[16,32,128]{2,1,0:T(8,128)(2,1)S(1)}, bf16[16,32,128]{2,1,0:T(8,128)(2,1)S(1)}, u32[]{:S(2)}, u32[]{:S(2)}) %collective-permute-start.4) | collective-permute-done | bytes 131104 | tf_op jit(solution)/shard_map/ppermute | solution.py:332
  57.4 0.0 copy-done
  57.4 3.0 %late.1 = bf16[2,16,16,2,384]{4,3,2,1,0:T(2,128)(2,1)} custom-call(f32[8,256,256]{2,1,0:T(8,128)S(1)} %early.1.sums_ref, bf16[16,32,128]{2,1,0:T(8,128)(2,1)S(1)} %collective-permute-done.4.far_ref, bf16[192,160]{1,0:T(8,128)(2,1)S(1)} %get-tuple-element.8.weight_ref, s32[1,128]{1,0:T(1,128)S(1)} %copy-done), custom_call_target="tpu_custom_call" | custom-call | tf_op jit(solution)/shard_map/late/pallas_call | solution.py:309
Async XLA Ops:
  22.4 21.1 %collective-permute-start.1 = (bf16[16,32,128]{2,1,0:T(8,128)(2,1)S(1)}, bf16[16,32,128]{2,1,0:T(8,128)(2,1)S(1)}, u32[]{:S(2)}, u32[]{:S(2)}) collective-permute-start(bf16[16,32,128]{2,1,0:T(8,128)(2,1)S(1)} %slab.1.own_ref), channel_id=1, source_target_pairs={{480,0},{64,32},{32,64},{128,96},{96,128},{192,160},{160,192},{256... | collective-permute-start | bytes 393224 | tf_op jit(solution)/shard_map/ppermute | solution.py:332
  34.3 14.9 %collective-permute-start = (bf16[16,32,128]{2,1,0:T(8,128)(2,1)S(1)}, bf16[16,32,128]{2,1,0:T(8,128)(2,1)S(1)}, u32[]{:S(2)}, u32[]{:S(2)}) collective-permute-start(bf16[16,32,128]{2,1,0:T(8,128)(2,1)S(1)} %slab.1.own_ref), channel_id=1, source_target_pairs={{32,0},{0,32},{96,64},{64,96},{160,128},{128,160},{224,192},{192,2... | collective-permute-start | bytes 393224 | tf_op jit(solution)/shard_map/ppermute | solution.py:332
  36.3 13.0 %collective-permute-start.2 = (bf16[16,32,128]{2,1,0:T(8,128)(2,1)S(1)}, bf16[16,32,128]{2,1,0:T(8,128)(2,1)S(1)}, u32[]{:S(2)}, u32[]{:S(2)}) collective-permute-start(bf16[16,32,128]{2,1,0:T(8,128)(2,1)S(1)} %slab.1.own_ref), channel_id=1, source_target_pairs={{480,0},{448,32},{416,64},{384,96},{352,128},{320,160},{288,192},{... | collective-permute-start | bytes 393224 | tf_op jit(solution)/shard_map/ppermute | solution.py:332
  38.4 10.8 %collective-permute-start.3 = (bf16[16,32,128]{2,1,0:T(8,128)(2,1)S(1)}, bf16[16,32,128]{2,1,0:T(8,128)(2,1)S(1)}, u32[]{:S(2)}, u32[]{:S(2)}) collective-permute-start(bf16[16,32,128]{2,1,0:T(8,128)(2,1)S(1)} %slab.1.own_ref), channel_id=1, source_target_pairs={{0,0},{416,32},{448,64},{352,96},{384,128},{288,160},{320,192},{22... | collective-permute-start | bytes 393224 | tf_op jit(solution)/shard_map/ppermute | solution.py:332
  39.1 1.0 %copy-start.1 = (bf16[2,6,16,6,32]{4,2,3,1,0:T(8,128)(2,1)S(1)}, bf16[2,6,16,6,32]{4,2,3,1,0:T(8,128)(2,1)}, u32[]{:S(2)}) copy-start(bf16[2,6,16,6,32]{4,2,3,1,0:T(8,128)(2,1)} %param.10) | copy-start | bytes 221188
  40.1 0.7 %copy-start.2 = (s32[6]{0:T(128)S(1)}, s32[6]{0:T(128)}, u32[]{:S(2)}) copy-start(s32[6]{0:T(128)} %ky_ref.1) | copy-start | bytes 76
  40.7 0.7 %copy-start.3 = (s32[6]{0:T(128)S(1)}, s32[6]{0:T(128)}, u32[]{:S(2)}) copy-start(s32[6]{0:T(128)} %kz_ref.1) | copy-start | bytes 76
  43.4 13.9 %collective-permute-start.4 = (bf16[16,32,128]{2,1,0:T(8,128)(2,1)S(1)}, bf16[16,32,128]{2,1,0:T(8,128)(2,1)S(1)}, u32[]{:S(2)}, u32[]{:S(2)}) collective-permute-start(bf16[16,32,128]{2,1,0:T(8,128)(2,1)S(1)} %collective-permute-done.1.next1_ref), channel_id=1, source_target_pairs={{416,0},{0,32},{352,64},{448,96},{288,128},{384,160},{224,192},{32... | collective-permute-start | bytes 393224 | tf_op jit(solution)/shard_map/ppermute | solution.py:332
  49.3 8.1 %copy-start = (s32[1,128]{1,0:T(1,128)S(1)}, s32[1,128]{1,0:T(1,128)}, u32[]{:S(2)}) copy-start(s32[1,128]{1,0:T(1,128)} %acquired_ref.1) | copy-start | bytes 1540

commit v4 on v3

--- a/solution.py
+++ b/solution.py
@@ -1,3 +1,4 @@
+import functools
 import math
 
 import jax
@@ -109,12 +110,10 @@
     )(lines, dft_table())
 
 
-def slab_kernel(in_ref, out_ref, rows_ref):
+def slab_kernel(in_ref, place_ref, out_ref, rows_ref):
     rows_ref[...] = in_ref[...].reshape(GX * NXL, AL * SC).astype(F32)
     eye = column_onehot(iota((128, 1), 0), 128)
     group = 128 // GX
-    k = iota((AL * 128, 1), 0)
-    place = column_onehot((k % 128) // GX * NY3 + (k % GX) * AL + k // 128, group * NY3)
     flats = []
     for part in range(NXL // group):
         rows = jnp.concatenate(
@@ -124,7 +123,7 @@
         flats.append(
             jnp.concatenate([turned[al * SC : (al + 1) * SC] for al in range(AL)], axis=1)
         )
-    spread = dot(jnp.concatenate(flats, axis=0), place).astype(BF16)
+    spread = dot(jnp.concatenate(flats, axis=0), place_ref[...]).astype(BF16)
     for part in range(NXL // group):
         for x in range(group):
             out_ref[part * group + x] = spread[
@@ -132,19 +131,36 @@
             ]
 
 
-def to_slab(lines):
+def to_slab(lines, place):
     return pl.pallas_call(
         slab_kernel,
         out_shape=jax.ShapeDtypeStruct((NXL, SC, NY3), BF16),
         scratch_shapes=[pltpu.VMEM((GX * NXL, AL * SC), F32)],
         compiler_params=room(8),
         name="slab",
-    )(lines)
+    )(lines, place)
+
+
+def make_tables(place_ref, moves_ref, weave_ref):
+    group = 128 // GX
+    k = iota((AL * 128, 1), 0)
+    place_ref[...] = column_onehot(
+        (k % 128) // GX * NY3 + (k % GX) * AL + k // 128, group * NY3
+    )
+    k = iota((NY3, 1), 0)
+    for d in range(SHIFTS):
+        lanes = slice(d * NY3, (d + 1) * NY3)
+        moves_ref[0, :, lanes] = column_onehot(k - (d - 2), NY3)
+        moves_ref[1, :, lanes] = column_onehot(NY3 - 1 - k - (d - 2), NY3)
+    k = iota((3 * NY3, 1), 0)
+    weave_ref[...] = column_onehot((k % NY3) * 3 + k // NY3, 3 * NY3)
 
 
 def weights_kernel(
-    ky_ref, kz_ref, kernels_ref, out_ref, far_ref, wide_ref, placed_ref, placed_far_ref
+    ky_ref, kz_ref, kernels_ref, out_ref, far_ref, place_ref, moves_ref, weave_ref,
+    wide_ref, placed_ref, placed_far_ref,
 ):
+    make_tables(place_ref, moves_ref, weave_ref)
     direct, crossed = [], []
     for t in range(6):
         for p in range(6):
@@ -206,6 +222,9 @@
         out_shape=(
             jax.ShapeDtypeStruct((8 * SC, KPAD), BF16),
             jax.ShapeDtypeStruct((6 * SC, KFAR), BF16),
+            jax.ShapeDtypeStruct((AL * 128, 128 // GX * NY3), BF16),
+            jax.ShapeDtypeStruct((2, NY3, SHIFTS * NY3), BF16),
+            jax.ShapeDtypeStruct((3 * NY3, 3 * NY3), BF16),
         ),
         in_specs=[smem, smem, vmem],
         scratch_shapes=[
@@ -219,71 +238,85 @@
     )(ky_start, kz_start, kernels.transpose(0, 1, 3, 2, 4))
 
 
-def spread(source_ref, slab, mirrored, at_of):
-    k = iota((NY3, 1), 0)
-    lane = iota((NY3, SHIFTS * NY3), 1)
-    want = lane % NY3 + lane // NY3 - 2
-    moves = onehot((NY3 - 1 - k if mirrored else k) == want)
-    moved = dot(slab.reshape(NXL * SC, NY3), moves).astype(BF16)
+def spread(source_ref, slab, moves, at_of):
+    count = slab.shape[0]
+    moved = dot(slab.reshape(count * SC, NY3), moves).astype(BF16)
     for d in range(SHIFTS):
-        for x in range(NXL):
+        for x in range(count):
             source_ref[x // 2, pl.ds(at_of(d), SC), (x % 2) * NY3 : (x % 2 + 1) * NY3] = moved[
                 x * SC : (x + 1) * SC, d * NY3 : (d + 1) * NY3
             ]
 
 
-def early_kernel(
-    own_ref, next0_ref, next1_ref, mirror_ref, near_ref, weight_ref, sums_ref, source_ref
-):
+def at(row, v):
+    return lambda d: pl.multiple_of(((row * SHIFTS + d) * 2 + v) * SC, SC)
+
+
+def early_kernel(own_ref, next0_ref, next1_ref, moves_ref, source_ref):
     odd = lax.axis_index("kz") % 2
-
-    def at(row, v):
-        return lambda d: pl.multiple_of(((row * SHIFTS + d) * 2 + v) * SC, SC)
-
     first, last = 2 * odd, 2 - 2 * odd
     for d in range(SHIFTS):
         for pair in range(NXL // 2):
             source_ref[pair, pl.ds(at(last, 1)(d), SC), :] = jnp.zeros((SC, 2 * NY3), BF16)
-    spread(source_ref, own_ref[...], False, at(1, 0))
-    spread(source_ref, next1_ref[...], False, at(first, 0))
-    spread(source_ref, near_ref[...], True, at(first, 1))
-    spread(source_ref, mirror_ref[...], True, at(1, 1))
-    spread(source_ref, next0_ref[...], False, at(last, 0))
+    spread(source_ref, own_ref[...], moves_ref[0], at(1, 0))
+    spread(source_ref, next1_ref[...], moves_ref[0], at(first, 0))
+    spread(source_ref, next0_ref[...], moves_ref[0], at(last, 0))
+
+
+def middle_kernel(near_ref, weight_ref, moves_ref, _, sums_ref, source_ref):
+    spread(source_ref, near_ref[0], moves_ref[1], at(2 * (lax.axis_index("kz") % 2), 1))
+    spread(source_ref, near_ref[1], moves_ref[1], at(1, 1))
     weights = weight_ref[:, :KDIM]
     for pair in range(NXL // 2):
         sums_ref[pair] = dot(weights, source_ref[pair])
 
 
-def early(slabs, weights):
-    return pl.pallas_call(
+def early(slabs, near, weights, moves):
+    vmem = pl.BlockSpec(memory_space=pltpu.VMEM)
+    source = jax.ShapeDtypeStruct((NXL // 2, KDIM, 2 * NY3), BF16)
+    spread_out = pl.pallas_call(
         early_kernel,
-        out_shape=jax.ShapeDtypeStruct((NXL // 2, 8 * SC, 2 * NY3), F32),
-        scratch_shapes=[pltpu.VMEM((NXL // 2, KDIM, 2 * NY3), BF16)],
+        out_shape=source,
+        in_specs=[vmem] * 4,
+        out_specs=vmem,
+        compiler_params=room(12),
+        cost_estimate=pl.CostEstimate(
+            flops=500_000_000, bytes_accessed=4_000_000, transcendentals=0
+        ),
+        name="early",
+    )(*slabs, moves)
+    return pl.pallas_call(
+        middle_kernel,
+        out_shape=(jax.ShapeDtypeStruct((NXL // 2, 8 * SC, 2 * NY3), F32), source),
+        in_specs=[vmem] * 4,
+        out_specs=(vmem, vmem),
+        input_output_aliases={3: 1},
         compiler_params=room(16),
         cost_estimate=pl.CostEstimate(
-            flops=1_500_000_000, bytes_accessed=4_000_000, transcendentals=0
+            flops=1_000_000_000, bytes_accessed=4_000_000, transcendentals=0
         ),
-        name="early",
-    )(*slabs, weights)
+        name="middle",
+    )(near, weights, moves, spread_out)[0]
 
 
 def late_kernel(
-    sums_ref, far_ref, weight_ref, acquired_ref, out_hbm, source_ref, out_ref, sems
+    start, sums_ref, far_ref, weight_ref, moves_ref, weave_ref, acquired_ref, *rest
 ):
-    spread(source_ref, far_ref[...], True, lambda d: d * SC)
+    out_hbm, source_ref, out_ref, sems = rest[-4:]
+    spread(source_ref, far_ref[...], moves_ref[1], lambda d: d * SC)
     weights = weight_ref[...]
     acquired = acquired_ref[...]
-    n = iota((3 * NY3, 1), 0)
-    weave = column_onehot((n % NY3) * 3 + n // NY3, 3 * NY3)
+    weave = weave_ref[...]
     parity = iota((2 * SC, NY3), 0) % 2
     masks = [jnp.broadcast_to(acquired, (2 * SC, NY3)) == 2 * ry + parity for ry in range(3)]
     copies = []
-    for pair in range(NXL // 2):
-        result = dot(weights, source_ref[pair]) + sums_ref[pair, : 6 * SC]
+    for pair in range(NXL // 4):
+        full = start + pair
+        result = dot(weights, source_ref[pair]) + sums_ref[full, : 6 * SC]
         lines = []
         for half in range(2):
             lanes = slice(half * NY3, (half + 1) * NY3)
-            kept = sums_ref[pair, 6 * SC :, lanes]
+            kept = sums_ref[full, 6 * SC :, lanes]
             chosen = [
                 jnp.where(masks[ry], kept, result[ry * 2 * SC : (ry + 1) * 2 * SC, lanes])
                 for ry in range(3)
@@ -295,37 +328,41 @@
                 at = (half * 2 + s) * SC
                 out_ref[s, 2 * pair + half] = woven[at : at + SC].reshape(COILS, 2, 3 * NY3)
         for s in range(2):
-            two = pl.ds(2 * pair, 2)
-            copy = pltpu.make_async_copy(out_ref.at[s, two], out_hbm.at[s, two], sems.at[s, pair])
+            copy = pltpu.make_async_copy(
+                out_ref.at[s, pl.ds(2 * pair, 2)], out_hbm.at[s, pl.ds(2 * full, 2)], sems.at[s, pair]
+            )
             copy.start()
             copies.append(copy)
     for copy in copies:
         copy.wait()
 
 
-def late(sums, far, weights, acquired_at):
+def late(half, filled, sums, far, weights, moves, weave, acquired_at):
     vmem = pl.BlockSpec(memory_space=pltpu.VMEM)
+    hbm = pl.BlockSpec(memory_space=pltpu.HBM)
     shape = (2, NXL, COILS, 2, 3 * NY3)
     return pl.pallas_call(
-        late_kernel,
+        functools.partial(late_kernel, half * NXL // 4),
         out_shape=jax.ShapeDtypeStruct(shape, BF16),
-        in_specs=[vmem] * 4,
-        out_specs=pl.BlockSpec(memory_space=pltpu.HBM),
+        in_specs=[vmem] * 6 + [hbm] * len(filled),
+        out_specs=hbm,
+        input_output_aliases={6: 0} if filled else {},
         scratch_shapes=[
-            pltpu.VMEM((NXL // 2, KFAR, 2 * NY3), BF16),
-            pltpu.VMEM(shape, BF16),
-            pltpu.SemaphoreType.DMA((2, NXL // 2)),
+            pltpu.VMEM((NXL // 4, KFAR, 2 * NY3), BF16),
+            pltpu.VMEM((2, NXL // 2, COILS, 2, 3 * NY3), BF16),
+            pltpu.SemaphoreType.DMA((2, NXL // 4)),
         ],
         compiler_params=room(16),
-        name="late",
-    )(sums, far, weights, acquired_at)
+    )(sums, far, weights, moves, weave, acquired_at, *filled)
 
 
 def local(kspace_lines, acquired_at, ky_start, kz_start, kernels):
     spectra = dft(kspace_lines)
     gathered = lax.all_to_all(spectra, "gx", split_axis=0, concat_axis=0, tiled=True)
-    weights, far_weights = placed_weights(kernels, ky_start, kz_start)
-    own = to_slab(gathered)
+    weights, far_weights, place, moves, weave = placed_weights(
+        kernels, ky_start, kz_start
+    )
+    own = to_slab(gathered, place)
 
     def fetch(values, source_of):
         pairs = [(source_of(b) % NZC, b) for b in range(NZC)]
@@ -333,11 +370,12 @@
 
     next1 = fetch(own, lambda b: b - 1 + 2 * (b % 2))
     next0 = fetch(own, lambda b: b + 1 - 2 * (b % 2))
-    near = fetch(own, lambda b: NZC - 2 * (b % 2) - b)
-    mirror = fetch(own, lambda b: NZC - 1 - b)
-    far = fetch(next1, lambda b: NZC - 3 + 4 * (b % 2) - b)
-    sums = early((own, next0, next1, mirror, near), weights)
-    return late(sums, far, far_weights, acquired_at)
+    near = fetch(jnp.stack([own, next1]), lambda b: NZC - 2 * (b % 2) - b)
+    far0 = fetch(next1[: NXL // 2], lambda b: NZC - 3 + 4 * (b % 2) - b)
+    far1 = fetch(next1[NXL // 2 :], lambda b: NZC - 3 + 4 * (b % 2) - b)
+    sums = early((own, next0, next1), near, weights, moves)
+    first = late(0, (), sums, far0, far_weights, moves, weave, acquired_at)
+    return late(1, (first,), sums, far1, far_weights, moves, weave, acquired_at)
 
 
 def solution(mesh):

time: 60.7 us -> 56.3 us (0.928)
  blocking collectives: 19.8 us -> 0 us
  starting transfers between devices: 22.5 us -> 33.6 us
  waiting for transfers between devices: 5.72 us -> 8.52 us
  Pallas kernels: 9.94 us -> 11.1 us
    all_to_all x1 -> x0, blocking collectives: 19.8 us -> none  [local(): lax.all_to_all(spectra, 'gx', split_axis=0, concat_axis=0, tiled=True)]
    all_to_all x0 -> x1, starting transfers between devices: none -> 10.6 us  [local(): lax.all_to_all(spectra, 'gx', split_axis=0, concat_axis=0, tiled=True)]
    all_to_all x0 -> x1, waiting for transfers between devices: none -> 4.69 us  [local(): lax.all_to_all(spectra, 'gx', split_axis=0, concat_axis=0, tiled=True)]
    ppermute x5, waiting for transfers between devices: 5.72 us -> 3.83 us  [fetch(): return lax.ppermute(values, 'kz', pairs)]
    pallas_call x2 -> x4, Pallas kernels: 5.35 us -> 6.31 us  [the longest x2 3.93 us: late(): pl.pallas_call(functools.partial(late_kernel, half * NXL // 4), out_shape...]
  transfers between devices with their start and end apart: 5 -> 6, of which waited for: 1 -> 2; matrix products, arithmetic and copies ran while one was open for 0% -> 0% of each run, Pallas kernels for 7% -> 12%
where the time goes in v4:
time: 56.3 us; the launch traced here: 55.7 us
  starting transfers between devices  33.6 us (60%)
  Pallas kernels  11.1 us (20%)
  waiting for transfers between devices  8.52 us (15%)
  local copies, waits for them, and re-layouts  2.28 us (4%)
    ppermute x5, starting transfers between devices, fetch(): return lax.ppermute(values, 'kz', pairs)  23.1 us
    all_to_all x1, starting transfers between devices, local(): lax.all_to_all(spectra, 'gx', split_axis=0, concat_axis=0, tiled=True)  10.6 us
    all_to_all x1, waiting for transfers between devices, local(): lax.all_to_all(spectra, 'gx', split_axis=0, concat_axis=0, tiled=True)  4.69 us
    pallas_call x2, Pallas kernels, late(): pl.pallas_call(functools.partial(late_kernel, half * NXL // 4), out_shape...  3.93 us
    ppermute x5, waiting for transfers between devices, fetch(): return lax.ppermute(values, 'kz', pairs)  3.83 us
    unnamed x8, local copies, waits for them, and re-layouts  2.27 us
    pallas_call x1, Pallas kernels, placed_weights(): pl.pallas_call(weights_kernel, out_shape=(jax.ShapeDtypeStruct((8 * SC, K...  2.26 us
    pallas_call x1, Pallas kernels, dft(): pl.pallas_call(dft_kernel, out_shape=jax.ShapeDtypeStruct((GX, NXL, COILS...  2.13 us
  transfers between devices with their start and end apart: 6, of which 2 were waited for; matrix products, arithmetic and copies ran while one was open for 0% of the time, Pallas kernels for 12%

profile of v4, /device:TPU:1, one launch (start us, length us, event | category | flops | bytes accessed | tf_op | source)
XLA Modules:
  0.0 55.7 jit_solution(4628564110446139727)
XLA Ops:
  0.0 2.1 %dft.1 = bf16[32,16,128]{2,1,0:T(8,128)(2,1)} custom-call(bf16[16,1,4,2,512]{4,3,2,1,0:T(2,128)(2,1)} %lines_hbm.1, bf16[256,512]{1,0:T(8,128)(2,1)} %constant.5.table_hbm), custom_call_target="tpu_custom_call" | custom-call | tf_op jit(solution)/shard_map/dft/pallas_call | solution.py:99
  2.1 10.6 %all-to-all-start = ((bf16[32,16,128]{2,1,0:T(8,128)(2,1)}), bf16[32,16,128]{2,1,0:T(8,128)(2,1)S(1)}, u32[]{:S(2)}, u32[]{:S(2)}) async-start(bf16[32,16,128]{2,1,0:T(8,128)(2,1)} %dft.1), calls=%async_computation | async-start | bytes 262144 | tf_op jit(solution)/shard_map/all_to_all | solution.py:361
  12.7 0.0 copy-start.1
  12.7 1.0 %copy-done.1 = bf16[2,6,16,6,32]{4,2,3,1,0:T(8,128)(2,1)S(1)} copy-done((bf16[2,6,16,6,32]{4,2,3,1,0:T(8,128)(2,1)S(1)}, bf16[2,6,16,6,32]{4,2,3,1,0:T(8,128)(2,1)}, u32[]{:S(2)}) %copy-start.1) | copy-done | bytes 73752
  13.7 0.0 copy-start.2
  13.7 0.7 %copy-done.2 = s32[6]{0:T(128)S(1)} copy-done((s32[6]{0:T(128)S(1)}, s32[6]{0:T(128)}, u32[]{:S(2)}) %copy-start.2) | copy-done | bytes 48
  14.3 0.0 copy-start.3
  14.3 0.7 %copy-done.3 = s32[6]{0:T(128)S(1)} copy-done((s32[6]{0:T(128)S(1)}, s32[6]{0:T(128)}, u32[]{:S(2)}) %copy-start.3) | copy-done | bytes 48
  15.0 2.3 %weights.1 = (bf16[256,1024]{1,0:T(8,128)(2,1)S(1)}, bf16[192,160]{1,0:T(8,128)(2,1)S(1)}, bf16[512,512]{1,0:T(8,128)(2,1)S(1)}, bf16[2,128,640]{2,1,0:T(8,128)(2,1)S(1)}, bf16[384,384]{1,0:T(8,128)(2,1)S(1)}) custom-call(s32[6]{0:T(128)S(1)} %copy-done.2, s32[6]{0:T(128)S(1)} %copy-done.3, bf16[2,6,6,16,32]{4,3,2,1,0:T(8,128)(2,1)S(1)} %bitcast.5), custom_call_target="tpu_custom_call" | custom-call | flops 100000000 | bytes 4000000 | tf_op jit(solution)/shard_map/weights/pallas_call | solution.py:220
  17.3 4.7 %all-to-all-done.in_ref = bf16[32,16,128]{2,1,0:T(8,128)(2,1)S(1)} async-done(((bf16[32,16,128]{2,1,0:T(8,128)(2,1)}), bf16[32,16,128]{2,1,0:T(8,128)(2,1)S(1)}, u32[]{:S(2)}, u32[]{:S(2)}) %all-to-all-start) | async-done | bytes 131104 | tf_op jit(solution)/shard_map/all_to_all | solution.py:361
  21.9 0.4 slab.1.own_ref
  22.3 11.9 %collective-permute-start = (bf16[16,32,128]{2,1,0:T(8,128)(2,1)S(1)}, bf16[16,32,128]{2,1,0:T(8,128)(2,1)S(1)}, u32[]{:S(2)}, u32[]{:S(2)}) collective-permute-start(bf16[16,32,128]{2,1,0:T(8,128)(2,1)S(1)} %slab.1.own_ref), channel_id=1, source_target_pairs={{480,0},{64,32},{32,64},{128,96},{96,128},{192,160},{160,192},{256... | collective-permute-start | bytes 393224 | tf_op jit(solution)/shard_map/ppermute | solution.py:369
  34.3 1.9 %collective-permute-start.2 = (bf16[16,32,128]{2,1,0:T(8,128)(2,1)S(1)}, bf16[16,32,128]{2,1,0:T(8,128)(2,1)S(1)}, u32[]{:S(2)}, u32[]{:S(2)}) collective-permute-start(bf16[16,32,128]{2,1,0:T(8,128)(2,1)S(1)} %slab.1.own_ref), channel_id=1, source_target_pairs={{32,0},{0,32},{96,64},{64,96},{160,128},{128,160},{224,192},{192,2... | collective-permute-start | bytes 393224 | tf_op jit(solution)/shard_map/ppermute | solution.py:369
  36.2 3.8 %collective-permute-done.next1_ref = bf16[16,32,128]{2,1,0:T(8,128)(2,1)S(1)} collective-permute-done((bf16[16,32,128]{2,1,0:T(8,128)(2,1)S(1)}, bf16[16,32,128]{2,1,0:T(8,128)(2,1)S(1)}, u32[]{:S(2)}, u32[]{:S(2)}) %collective-permute-start) | collective-permute-done | bytes 131104 | tf_op jit(solution)/shard_map/ppermute | solution.py:369
  40.1 0.7 %collective-permute-start.1 = (bf16[2,16,32,128]{3,2,1,0:T(8,128)(2,1)S(1)}, bf16[2,16,32,128]{3,2,1,0:T(8,128)(2,1)S(1)}, u32[]{:S(2)}, u32[]{:S(2)}) collective-permute-start(bf16[2,16,32,128]{3,2,1,0:T(8,128)(2,1)S(1)} %pad_maximum_fusion), channel_id=1, source_target_pairs={{0,0},{416,32},{448,64},{352,96},{384,128},{288,160},{320,192},{22... | collective-permute-start | bytes 786440 | tf_op jit(solution)/shard_map/ppermute | solution.py:369
  40.8 4.4 %collective-permute-start.4 = (bf16[8,32,128]{2,1,0:T(8,128)(2,1)S(1)}, bf16[8,32,128]{2,1,0:T(8,128)(2,1)S(1)}, u32[]{:S(2)}, u32[]{:S(2)}) collective-permute-start(bf16[8,32,128]{2,1,0:T(8,128)(2,1)S(1)} %get-tuple-element.17), channel_id=1, source_target_pairs={{416,0},{0,32},{352,64},{448,96},{288,128},{384,160},{224,192},{32... | collective-permute-start | bytes 196616 | tf_op jit(solution)/shard_map/ppermute | solution.py:369
  45.2 4.1 %collective-permute-start.3 = (bf16[8,32,128]{2,1,0:T(8,128)(2,1)S(1)}, bf16[8,32,128]{2,1,0:T(8,128)(2,1)S(1)}, u32[]{:S(2)}, u32[]{:S(2)}) collective-permute-start(bf16[8,32,128]{2,1,0:T(8,128)(2,1)S(1)} %get-tuple-element.18), channel_id=1, source_target_pairs={{416,0},{0,32},{352,64},{448,96},{288,128},{384,160},{224,192},{32... | collective-permute-start | bytes 196616 | tf_op jit(solution)/shard_map/ppermute | solution.py:369
  49.3 0.0 collective-permute-done.2.next0_ref
  49.3 0.0 copy-start
  49.3 0.7 %early.1._ = bf16[8,960,256]{2,1,0:T(8,128)(2,1)S(1)} custom-call(bf16[16,32,128]{2,1,0:T(8,128)(2,1)S(1)} %slab.1.own_ref, bf16[16,32,128]{2,1,0:T(8,128)(2,1)S(1)} %collective-permute-done.2.next0_ref, bf16[16,32,128]{2,1,0:T(8,128)(2,1)S(1)} %collective-permute-done.next1_ref, bf16[2,128,640]{2,1,0:T(8,128)(2,1)S(1)} %get-tuple-element.13.moves_ref), custom_call_target="tpu_custom_call" | custom-call | flops 500000000 | bytes 4000000 | tf_op jit(solution)/shard_map/early/pallas_call | solution.py:277
  50.1 0.0 collective-permute-done.1.near_ref
  50.1 1.7 %middle.1 = (f32[8,256,256]{2,1,0:T(8,128)S(1)}, bf16[8,960,256]{2,1,0:T(8,128)(2,1)S(1)}) custom-call(bf16[2,16,32,128]{3,2,1,0:T(8,128)(2,1)S(1)} %collective-permute-done.1.near_ref, bf16[256,1024]{1,0:T(8,128)(2,1)S(1)} %get-tuple-element.12.weight_ref, bf16[2,128,640]{2,1,0:T(8,128)(2,1)S(1)} %get-tuple-element.13.moves_ref, ...), custom_call_target="tpu_custom_call", output_to_operand_aliasing={{1}: (3, {})} | custom-call | flops 1000000000 | bytes 4000000 | tf_op jit(solution)/shard_map/middle/pallas_call | solution.py:288
  51.7 0.0 collective-permute-done.4.far_ref
  51.8 0.0 copy-done
  51.8 2.0 %shard_map.64.rest_0_ = bf16[2,16,16,2,384]{4,3,2,1,0:T(2,128)(2,1)} custom-call(f32[8,256,256]{2,1,0:T(8,128)S(1)} %get-tuple-element.14.sums_ref, bf16[8,32,128]{2,1,0:T(8,128)(2,1)S(1)} %collective-permute-done.4.far_ref, bf16[192,160]{1,0:T(8,128)(2,1)S(1)} %get-tuple-element.15.weight_ref, bf16[2,128,640]{2,1,0:T(8,128)(2,1)S(1)} %get-tuple-element.13.moves_ref, ...), custom_call_target="tpu_custom_call" | custom-call | tf_op jit(solution)/shard_map/pallas_call | solution.py:344
  53.7 0.0 collective-permute-done.3.far_ref
  53.7 2.0 %shard_map.65 = bf16[2,16,16,2,384]{4,3,2,1,0:T(2,128)(2,1)} custom-call(f32[8,256,256]{2,1,0:T(8,128)S(1)} %get-tuple-element.14.sums_ref, bf16[8,32,128]{2,1,0:T(8,128)(2,1)S(1)} %collective-permute-done.3.far_ref, bf16[192,160]{1,0:T(8,128)(2,1)S(1)} %get-tuple-element.15.weight_ref, ...), custom_call_target="tpu_custom_call", output_to_operand_aliasing={{}: (6, {})} | custom-call | tf_op jit(solution)/shard_map/pallas_call | solution.py:344
  (2 shorter events, 0.0 us)
Async XLA Ops:
  2.1 19.8 %all-to-all-start = ((bf16[32,16,128]{2,1,0:T(8,128)(2,1)}), bf16[32,16,128]{2,1,0:T(8,128)(2,1)S(1)}, u32[]{:S(2)}, u32[]{:S(2)}) async-start(bf16[32,16,128]{2,1,0:T(8,128)(2,1)} %dft.1), calls=%async_computation | async-start | bytes 262144 | tf_op jit(solution)/shard_map/all_to_all | solution.py:361
  12.7 1.0 %copy-start.1 = (bf16[2,6,16,6,32]{4,2,3,1,0:T(8,128)(2,1)S(1)}, bf16[2,6,16,6,32]{4,2,3,1,0:T(8,128)(2,1)}, u32[]{:S(2)}) copy-start(bf16[2,6,16,6,32]{4,2,3,1,0:T(8,128)(2,1)} %param.10) | copy-start | bytes 221188
  13.7 0.7 %copy-start.2 = (s32[6]{0:T(128)S(1)}, s32[6]{0:T(128)}, u32[]{:S(2)}) copy-start(s32[6]{0:T(128)} %ky_ref.1) | copy-start | bytes 76
  14.3 0.7 %copy-start.3 = (s32[6]{0:T(128)S(1)}, s32[6]{0:T(128)}, u32[]{:S(2)}) copy-start(s32[6]{0:T(128)} %kz_ref.1) | copy-start | bytes 76
  22.3 17.7 %collective-permute-start = (bf16[16,32,128]{2,1,0:T(8,128)(2,1)S(1)}, bf16[16,32,128]{2,1,0:T(8,128)(2,1)S(1)}, u32[]{:S(2)}, u32[]{:S(2)}) collective-permute-start(bf16[16,32,128]{2,1,0:T(8,128)(2,1)S(1)} %slab.1.own_ref), channel_id=1, source_target_pairs={{480,0},{64,32},{32,64},{128,96},{96,128},{192,160},{160,192},{256... | collective-permute-start | bytes 393224 | tf_op jit(solution)/shard_map/ppermute | solution.py:369
  34.3 15.0 %collective-permute-start.2 = (bf16[16,32,128]{2,1,0:T(8,128)(2,1)S(1)}, bf16[16,32,128]{2,1,0:T(8,128)(2,1)S(1)}, u32[]{:S(2)}, u32[]{:S(2)}) collective-permute-start(bf16[16,32,128]{2,1,0:T(8,128)(2,1)S(1)} %slab.1.own_ref), channel_id=1, source_target_pairs={{32,0},{0,32},{96,64},{64,96},{160,128},{128,160},{224,192},{192,2... | collective-permute-start | bytes 393224 | tf_op jit(solution)/shard_map/ppermute | solution.py:369
  40.1 10.0 %collective-permute-start.1 = (bf16[2,16,32,128]{3,2,1,0:T(8,128)(2,1)S(1)}, bf16[2,16,32,128]{3,2,1,0:T(8,128)(2,1)S(1)}, u32[]{:S(2)}, u32[]{:S(2)}) collective-permute-start(bf16[2,16,32,128]{3,2,1,0:T(8,128)(2,1)S(1)} %pad_maximum_fusion), channel_id=1, source_target_pairs={{0,0},{416,32},{448,64},{352,96},{384,128},{288,160},{320,192},{22... | collective-permute-start | bytes 786440 | tf_op jit(solution)/shard_map/ppermute | solution.py:369
  40.8 11.0 %collective-permute-start.4 = (bf16[8,32,128]{2,1,0:T(8,128)(2,1)S(1)}, bf16[8,32,128]{2,1,0:T(8,128)(2,1)S(1)}, u32[]{:S(2)}, u32[]{:S(2)}) collective-permute-start(bf16[8,32,128]{2,1,0:T(8,128)(2,1)S(1)} %get-tuple-element.17), channel_id=1, source_target_pairs={{416,0},{0,32},{352,64},{448,96},{288,128},{384,160},{224,192},{32... | collective-permute-start | bytes 196616 | tf_op jit(solution)/shard_map/ppermute | solution.py:369
  45.2 8.5 %collective-permute-start.3 = (bf16[8,32,128]{2,1,0:T(8,128)(2,1)S(1)}, bf16[8,32,128]{2,1,0:T(8,128)(2,1)S(1)}, u32[]{:S(2)}, u32[]{:S(2)}) collective-permute-start(bf16[8,32,128]{2,1,0:T(8,128)(2,1)S(1)} %get-tuple-element.18), channel_id=1, source_target_pairs={{416,0},{0,32},{352,64},{448,96},{288,128},{384,160},{224,192},{32... | collective-permute-start | bytes 196616 | tf_op jit(solution)/shard_map/ppermute | solution.py:369
  49.3 2.4 %copy-start = (s32[1,128]{1,0:T(1,128)S(1)}, s32[1,128]{1,0:T(1,128)}, u32[]{:S(2)}) copy-start(s32[1,128]{1,0:T(1,128)} %acquired_ref.3) | copy-start | bytes 1540

commit v5 on v3

--- a/solution.py
+++ b/solution.py
@@ -109,12 +109,10 @@
     )(lines, dft_table())
 
 
-def slab_kernel(in_ref, out_ref, rows_ref):
+def slab_kernel(in_ref, place_ref, out_ref, rows_ref):
     rows_ref[...] = in_ref[...].reshape(GX * NXL, AL * SC).astype(F32)
     eye = column_onehot(iota((128, 1), 0), 128)
     group = 128 // GX
-    k = iota((AL * 128, 1), 0)
-    place = column_onehot((k % 128) // GX * NY3 + (k % GX) * AL + k // 128, group * NY3)
     flats = []
     for part in range(NXL // group):
         rows = jnp.concatenate(
@@ -124,7 +122,7 @@
         flats.append(
             jnp.concatenate([turned[al * SC : (al + 1) * SC] for al in range(AL)], axis=1)
         )
-    spread = dot(jnp.concatenate(flats, axis=0), place).astype(BF16)
+    spread = dot(jnp.concatenate(flats, axis=0), place_ref[...]).astype(BF16)
     for part in range(NXL // group):
         for x in range(group):
             out_ref[part * group + x] = spread[
@@ -132,19 +130,36 @@
             ]
 
 
-def to_slab(lines):
+def to_slab(lines, place):
     return pl.pallas_call(
         slab_kernel,
         out_shape=jax.ShapeDtypeStruct((NXL, SC, NY3), BF16),
         scratch_shapes=[pltpu.VMEM((GX * NXL, AL * SC), F32)],
         compiler_params=room(8),
         name="slab",
-    )(lines)
+    )(lines, place)
+
+
+def make_tables(place_ref, moves_ref, weave_ref):
+    group = 128 // GX
+    k = iota((AL * 128, 1), 0)
+    place_ref[...] = column_onehot(
+        (k % 128) // GX * NY3 + (k % GX) * AL + k // 128, group * NY3
+    )
+    k = iota((NY3, 1), 0)
+    for d in range(SHIFTS):
+        lanes = slice(d * NY3, (d + 1) * NY3)
+        moves_ref[0, :, lanes] = column_onehot(k - (d - 2), NY3)
+        moves_ref[1, :, lanes] = column_onehot(NY3 - 1 - k - (d - 2), NY3)
+    k = iota((3 * NY3, 1), 0)
+    weave_ref[...] = column_onehot((k % NY3) * 3 + k // NY3, 3 * NY3)
 
 
 def weights_kernel(
-    ky_ref, kz_ref, kernels_ref, out_ref, far_ref, wide_ref, placed_ref, placed_far_ref
+    ky_ref, kz_ref, kernels_ref, out_ref, far_ref, place_ref, moves_ref, weave_ref,
+    wide_ref, placed_ref, placed_far_ref,
 ):
+    make_tables(place_ref, moves_ref, weave_ref)
     direct, crossed = [], []
     for t in range(6):
         for p in range(6):
@@ -206,6 +221,9 @@
         out_shape=(
             jax.ShapeDtypeStruct((8 * SC, KPAD), BF16),
             jax.ShapeDtypeStruct((6 * SC, KFAR), BF16),
+            jax.ShapeDtypeStruct((AL * 128, 128 // GX * NY3), BF16),
+            jax.ShapeDtypeStruct((2, NY3, SHIFTS * NY3), BF16),
+            jax.ShapeDtypeStruct((3 * NY3, 3 * NY3), BF16),
         ),
         in_specs=[smem, smem, vmem],
         scratch_shapes=[
@@ -219,11 +237,7 @@
     )(ky_start, kz_start, kernels.transpose(0, 1, 3, 2, 4))
 
 
-def spread(source_ref, slab, mirrored, at_of):
-    k = iota((NY3, 1), 0)
-    lane = iota((NY3, SHIFTS * NY3), 1)
-    want = lane % NY3 + lane // NY3 - 2
-    moves = onehot((NY3 - 1 - k if mirrored else k) == want)
+def spread(source_ref, slab, moves, at_of):
     moved = dot(slab.reshape(NXL * SC, NY3), moves).astype(BF16)
     for d in range(SHIFTS):
         for x in range(NXL):
@@ -233,8 +247,10 @@
 
 
 def early_kernel(
-    own_ref, next0_ref, next1_ref, mirror_ref, near_ref, weight_ref, sums_ref, source_ref
+    own_ref, next0_ref, next1_ref, mirror_ref, near_ref, weight_ref, moves_ref, sums_ref,
+    source_ref,
 ):
+    straight, mirrored = moves_ref[0], moves_ref[1]
     odd = lax.axis_index("kz") % 2
 
     def at(row, v):
@@ -244,17 +260,17 @@
     for d in range(SHIFTS):
         for pair in range(NXL // 2):
             source_ref[pair, pl.ds(at(last, 1)(d), SC), :] = jnp.zeros((SC, 2 * NY3), BF16)
-    spread(source_ref, own_ref[...], False, at(1, 0))
-    spread(source_ref, next1_ref[...], False, at(first, 0))
-    spread(source_ref, near_ref[...], True, at(first, 1))
-    spread(source_ref, mirror_ref[...], True, at(1, 1))
-    spread(source_ref, next0_ref[...], False, at(last, 0))
+    spread(source_ref, own_ref[...], straight, at(1, 0))
+    spread(source_ref, next1_ref[...], straight, at(first, 0))
+    spread(source_ref, near_ref[...], mirrored, at(first, 1))
+    spread(source_ref, mirror_ref[...], mirrored, at(1, 1))
+    spread(source_ref, next0_ref[...], straight, at(last, 0))
     weights = weight_ref[:, :KDIM]
     for pair in range(NXL // 2):
         sums_ref[pair] = dot(weights, source_ref[pair])
 
 
-def early(slabs, weights):
+def early(slabs, weights, moves):
     return pl.pallas_call(
         early_kernel,
         out_shape=jax.ShapeDtypeStruct((NXL // 2, 8 * SC, 2 * NY3), F32),
@@ -264,17 +280,17 @@
             flops=1_500_000_000, bytes_accessed=4_000_000, transcendentals=0
         ),
         name="early",
-    )(*slabs, weights)
+    )(*slabs, weights, moves)
 
 
 def late_kernel(
-    sums_ref, far_ref, weight_ref, acquired_ref, out_hbm, source_ref, out_ref, sems
+    sums_ref, far_ref, weight_ref, moves_ref, weave_ref, acquired_ref, out_hbm,
+    source_ref, out_ref, sems,
 ):
-    spread(source_ref, far_ref[...], True, lambda d: d * SC)
+    spread(source_ref, far_ref[...], moves_ref[1], lambda d: d * SC)
     weights = weight_ref[...]
     acquired = acquired_ref[...]
-    n = iota((3 * NY3, 1), 0)
-    weave = column_onehot((n % NY3) * 3 + n // NY3, 3 * NY3)
+    weave = weave_ref[...]
     parity = iota((2 * SC, NY3), 0) % 2
     masks = [jnp.broadcast_to(acquired, (2 * SC, NY3)) == 2 * ry + parity for ry in range(3)]
     copies = []
@@ -303,13 +319,13 @@
         copy.wait()
 
 
-def late(sums, far, weights, acquired_at):
+def late(sums, far, weights, moves, weave, acquired_at):
     vmem = pl.BlockSpec(memory_space=pltpu.VMEM)
     shape = (2, NXL, COILS, 2, 3 * NY3)
     return pl.pallas_call(
         late_kernel,
         out_shape=jax.ShapeDtypeStruct(shape, BF16),
-        in_specs=[vmem] * 4,
+        in_specs=[vmem] * 6,
         out_specs=pl.BlockSpec(memory_space=pltpu.HBM),
         scratch_shapes=[
             pltpu.VMEM((NXL // 2, KFAR, 2 * NY3), BF16),
@@ -318,14 +334,16 @@
         ],
         compiler_params=room(16),
         name="late",
-    )(sums, far, weights, acquired_at)
+    )(sums, far, weights, moves, weave, acquired_at)
 
 
 def local(kspace_lines, acquired_at, ky_start, kz_start, kernels):
     spectra = dft(kspace_lines)
     gathered = lax.all_to_all(spectra, "gx", split_axis=0, concat_axis=0, tiled=True)
-    weights, far_weights = placed_weights(kernels, ky_start, kz_start)
-    own = to_slab(gathered)
+    weights, far_weights, place, moves, weave = placed_weights(
+        kernels, ky_start, kz_start
+    )
+    own = to_slab(gathered, place)
 
     def fetch(values, source_of):
         pairs = [(source_of(b) % NZC, b) for b in range(NZC)]
@@ -336,8 +354,8 @@
     near = fetch(own, lambda b: NZC - 2 * (b % 2) - b)
     mirror = fetch(own, lambda b: NZC - 1 - b)
     far = fetch(next1, lambda b: NZC - 3 + 4 * (b % 2) - b)
-    sums = early((own, next0, next1, mirror, near), weights)
-    return late(sums, far, far_weights, acquired_at)
+    sums = early((own, next0, next1, mirror, near), weights, moves)
+    return late(sums, far, far_weights, moves, weave, acquired_at)
 
 
 def solution(mesh):

time: 60.7 us -> 56.5 us (0.931)
  the two profiles are of different devices: /device:TPU:1 before, /device:TPU:8 now
where the time goes in v5:
time: 56.5 us; the launch traced here: 56.2 us
  starting transfers between devices  29.4 us (52%)
  waiting for transfers between devices  14.3 us (25%)
  Pallas kernels  10.1 us (18%)
  local copies, waits for them, and re-layouts  2.27 us (4%)
    ppermute x5, starting transfers between devices, fetch(): return lax.ppermute(values, 'kz', pairs)  19.9 us
    ppermute x5, waiting for transfers between devices, fetch(): return lax.ppermute(values, 'kz', pairs)  9.86 us
    all_to_all x1, starting transfers between devices, local(): lax.all_to_all(spectra, 'gx', split_axis=0, concat_axis=0, tiled=True)  9.52 us
    all_to_all x1, waiting for transfers between devices, local(): lax.all_to_all(spectra, 'gx', split_axis=0, concat_axis=0, tiled=True)  4.41 us
    pallas_call x1, Pallas kernels, late(): pl.pallas_call(late_kernel, out_shape=jax.ShapeDtypeStruct(shape, BF16),...  2.96 us
    pallas_call x1, Pallas kernels, early(): pl.pallas_call(early_kernel, out_shape=jax.ShapeDtypeStruct((NXL // 2, 8...  2.36 us
    unnamed x8, local copies, waits for them, and re-layouts  2.27 us
    pallas_call x1, Pallas kernels, placed_weights(): pl.pallas_call(weights_kernel, out_shape=(jax.ShapeDtypeStruct((8 * SC, K...  2.25 us
  transfers between devices with their start and end apart: 6, of which 4 were waited for; matrix products, arithmetic and copies ran while one was open for 0% of the time, Pallas kernels for 8%

profile of v5, /device:TPU:8, one launch (start us, length us, event | category | flops | bytes accessed | tf_op | source)
XLA Modules:
  0.0 56.2 jit_solution(8276135852740800796)
XLA Ops:
  0.0 2.1 %dft.1 = bf16[32,16,128]{2,1,0:T(8,128)(2,1)} custom-call(bf16[16,1,4,2,512]{4,3,2,1,0:T(2,128)(2,1)} %lines_hbm.1, bf16[256,512]{1,0:T(8,128)(2,1)} %constant.5.table_hbm), custom_call_target="tpu_custom_call" | custom-call | tf_op jit(solution)/shard_map/dft/pallas_call | solution.py:98
  2.1 9.5 %all-to-all-start = ((bf16[32,16,128]{2,1,0:T(8,128)(2,1)}), bf16[32,16,128]{2,1,0:T(8,128)(2,1)S(1)}, u32[]{:S(2)}, u32[]{:S(2)}) async-start(bf16[32,16,128]{2,1,0:T(8,128)(2,1)} %dft.1), calls=%async_computation | async-start | bytes 262144 | tf_op jit(solution)/shard_map/all_to_all | solution.py:342
  11.7 0.0 copy-start.1
  11.7 1.0 %copy-done.1 = bf16[2,6,16,6,32]{4,2,3,1,0:T(8,128)(2,1)S(1)} copy-done((bf16[2,6,16,6,32]{4,2,3,1,0:T(8,128)(2,1)S(1)}, bf16[2,6,16,6,32]{4,2,3,1,0:T(8,128)(2,1)}, u32[]{:S(2)}) %copy-start.1) | copy-done | bytes 73752
  12.6 0.0 copy-start.2
  12.6 0.7 %copy-done.2 = s32[6]{0:T(128)S(1)} copy-done((s32[6]{0:T(128)S(1)}, s32[6]{0:T(128)}, u32[]{:S(2)}) %copy-start.2) | copy-done | bytes 48
  13.3 0.0 copy-start.3
  13.3 0.7 %copy-done.3 = s32[6]{0:T(128)S(1)} copy-done((s32[6]{0:T(128)S(1)}, s32[6]{0:T(128)}, u32[]{:S(2)}) %copy-start.3) | copy-done | bytes 48
  14.0 2.3 %weights.1 = (bf16[256,1024]{1,0:T(8,128)(2,1)S(1)}, bf16[192,160]{1,0:T(8,128)(2,1)S(1)}, bf16[512,512]{1,0:T(8,128)(2,1)S(1)}, bf16[2,128,640]{2,1,0:T(8,128)(2,1)S(1)}, bf16[384,384]{1,0:T(8,128)(2,1)S(1)}) custom-call(s32[6]{0:T(128)S(1)} %copy-done.2, s32[6]{0:T(128)S(1)} %copy-done.3, bf16[2,6,6,16,32]{4,3,2,1,0:T(8,128)(2,1)S(1)} %bitcast.1), custom_call_target="tpu_custom_call" | custom-call | flops 100000000 | bytes 4000000 | tf_op jit(solution)/shard_map/weights/pallas_call | solution.py:219
  16.2 4.4 %all-to-all-done.in_ref = bf16[32,16,128]{2,1,0:T(8,128)(2,1)S(1)} async-done(((bf16[32,16,128]{2,1,0:T(8,128)(2,1)}), bf16[32,16,128]{2,1,0:T(8,128)(2,1)S(1)}, u32[]{:S(2)}, u32[]{:S(2)}) %all-to-all-start) | async-done | bytes 131104 | tf_op jit(solution)/shard_map/all_to_all | solution.py:342
  20.6 0.4 slab.1.own_ref
  21.0 12.2 %collective-permute-start.1 = (bf16[16,32,128]{2,1,0:T(8,128)(2,1)S(1)}, bf16[16,32,128]{2,1,0:T(8,128)(2,1)S(1)}, u32[]{:S(2)}, u32[]{:S(2)}) collective-permute-start(bf16[16,32,128]{2,1,0:T(8,128)(2,1)S(1)} %slab.1.own_ref), channel_id=1, source_target_pairs={{480,0},{64,32},{32,64},{128,96},{96,128},{192,160},{160,192},{256... | collective-permute-start | bytes 393224 | tf_op jit(solution)/shard_map/ppermute | solution.py:350
  33.3 1.9 %collective-permute-start = (bf16[16,32,128]{2,1,0:T(8,128)(2,1)S(1)}, bf16[16,32,128]{2,1,0:T(8,128)(2,1)S(1)}, u32[]{:S(2)}, u32[]{:S(2)}) collective-permute-start(bf16[16,32,128]{2,1,0:T(8,128)(2,1)S(1)} %slab.1.own_ref), channel_id=1, source_target_pairs={{32,0},{0,32},{96,64},{64,96},{160,128},{128,160},{224,192},{192,2... | collective-permute-start | bytes 393224 | tf_op jit(solution)/shard_map/ppermute | solution.py:350
  35.2 2.5 %collective-permute-start.2 = (bf16[16,32,128]{2,1,0:T(8,128)(2,1)S(1)}, bf16[16,32,128]{2,1,0:T(8,128)(2,1)S(1)}, u32[]{:S(2)}, u32[]{:S(2)}) collective-permute-start(bf16[16,32,128]{2,1,0:T(8,128)(2,1)S(1)} %slab.1.own_ref), channel_id=1, source_target_pairs={{480,0},{448,32},{416,64},{384,96},{352,128},{320,160},{288,192},{... | collective-permute-start | bytes 393224 | tf_op jit(solution)/shard_map/ppermute | solution.py:350
  37.7 0.7 %collective-permute-start.3 = (bf16[16,32,128]{2,1,0:T(8,128)(2,1)S(1)}, bf16[16,32,128]{2,1,0:T(8,128)(2,1)S(1)}, u32[]{:S(2)}, u32[]{:S(2)}) collective-permute-start(bf16[16,32,128]{2,1,0:T(8,128)(2,1)S(1)} %slab.1.own_ref), channel_id=1, source_target_pairs={{0,0},{416,32},{448,64},{352,96},{384,128},{288,160},{320,192},{22... | collective-permute-start | bytes 393224 | tf_op jit(solution)/shard_map/ppermute | solution.py:350
  38.3 3.8 %collective-permute-done.1.next1_ref = bf16[16,32,128]{2,1,0:T(8,128)(2,1)S(1)} collective-permute-done((bf16[16,32,128]{2,1,0:T(8,128)(2,1)S(1)}, bf16[16,32,128]{2,1,0:T(8,128)(2,1)S(1)}, u32[]{:S(2)}, u32[]{:S(2)}) %collective-permute-start.1) | collective-permute-done | bytes 131104 | tf_op jit(solution)/shard_map/ppermute | solution.py:350
  42.1 2.6 %collective-permute-start.4 = (bf16[16,32,128]{2,1,0:T(8,128)(2,1)S(1)}, bf16[16,32,128]{2,1,0:T(8,128)(2,1)S(1)}, u32[]{:S(2)}, u32[]{:S(2)}) collective-permute-start(bf16[16,32,128]{2,1,0:T(8,128)(2,1)S(1)} %collective-permute-done.1.next1_ref), channel_id=1, source_target_pairs={{416,0},{0,32},{352,64},{448,96},{288,128},{384,160},{224,192},{32... | collective-permute-start | bytes 393224 | tf_op jit(solution)/shard_map/ppermute | solution.py:350
  44.7 0.0 collective-permute-done.next0_ref
  44.7 1.8 %collective-permute-done.2.mirror_ref = bf16[16,32,128]{2,1,0:T(8,128)(2,1)S(1)} collective-permute-done((bf16[16,32,128]{2,1,0:T(8,128)(2,1)S(1)}, bf16[16,32,128]{2,1,0:T(8,128)(2,1)S(1)}, u32[]{:S(2)}, u32[]{:S(2)}) %collective-permute-start.2) | collective-permute-done | bytes 131104 | tf_op jit(solution)/shard_map/ppermute | solution.py:350
  46.6 0.0 collective-permute-done.3.near_ref
  46.6 0.0 copy-start
  46.6 2.4 %early.1.sums_ref = f32[8,256,256]{2,1,0:T(8,128)S(1)} custom-call(bf16[16,32,128]{2,1,0:T(8,128)(2,1)S(1)} %slab.1.own_ref, bf16[16,32,128]{2,1,0:T(8,128)(2,1)S(1)} %collective-permute-done.next0_ref, bf16[16,32,128]{2,1,0:T(8,128)(2,1)S(1)} %collective-permute-done.1.next1_ref, bf16[16,32,128]{2,1,0:T(8,128)(2,1)S(1)} %collective-permute-done.2.mirror_ref, ...), custom_call_target="tpu_custom_call" | custom-call | flops 1500000000 | bytes 4000000 | tf_op jit(solution)/shard_map/early/pallas_call | solution.py:274
  48.9 4.2 %collective-permute-done.4.far_ref = bf16[16,32,128]{2,1,0:T(8,128)(2,1)S(1)} collective-permute-done((bf16[16,32,128]{2,1,0:T(8,128)(2,1)S(1)}, bf16[16,32,128]{2,1,0:T(8,128)(2,1)S(1)}, u32[]{:S(2)}, u32[]{:S(2)}) %collective-permute-start.4) | collective-permute-done | bytes 131104 | tf_op jit(solution)/shard_map/ppermute | solution.py:350
  53.2 0.0 copy-done
  53.2 3.0 %late.1 = bf16[2,16,16,2,384]{4,3,2,1,0:T(2,128)(2,1)} custom-call(f32[8,256,256]{2,1,0:T(8,128)S(1)} %early.1.sums_ref, bf16[16,32,128]{2,1,0:T(8,128)(2,1)S(1)} %collective-permute-done.4.far_ref, bf16[192,160]{1,0:T(8,128)(2,1)S(1)} %get-tuple-element.13.weight_ref, bf16[2,128,640]{2,1,0:T(8,128)(2,1)S(1)} %get-tuple-element.12.moves_ref, ...), custom_call_target="tpu_custom_call" | custom-call | tf_op jit(solution)/shard_map/late/pallas_call | solution.py:325
Async XLA Ops:
  2.1 18.5 %all-to-all-start = ((bf16[32,16,128]{2,1,0:T(8,128)(2,1)}), bf16[32,16,128]{2,1,0:T(8,128)(2,1)S(1)}, u32[]{:S(2)}, u32[]{:S(2)}) async-start(bf16[32,16,128]{2,1,0:T(8,128)(2,1)} %dft.1), calls=%async_computation | async-start | bytes 262144 | tf_op jit(solution)/shard_map/all_to_all | solution.py:342
  11.7 1.0 %copy-start.1 = (bf16[2,6,16,6,32]{4,2,3,1,0:T(8,128)(2,1)S(1)}, bf16[2,6,16,6,32]{4,2,3,1,0:T(8,128)(2,1)}, u32[]{:S(2)}) copy-start(bf16[2,6,16,6,32]{4,2,3,1,0:T(8,128)(2,1)} %param.10) | copy-start | bytes 221188
  12.6 0.7 %copy-start.2 = (s32[6]{0:T(128)S(1)}, s32[6]{0:T(128)}, u32[]{:S(2)}) copy-start(s32[6]{0:T(128)} %ky_ref.1) | copy-start | bytes 76
  13.3 0.7 %copy-start.3 = (s32[6]{0:T(128)S(1)}, s32[6]{0:T(128)}, u32[]{:S(2)}) copy-start(s32[6]{0:T(128)} %kz_ref.1) | copy-start | bytes 76
  21.0 21.1 %collective-permute-start.1 = (bf16[16,32,128]{2,1,0:T(8,128)(2,1)S(1)}, bf16[16,32,128]{2,1,0:T(8,128)(2,1)S(1)}, u32[]{:S(2)}, u32[]{:S(2)}) collective-permute-start(bf16[16,32,128]{2,1,0:T(8,128)(2,1)S(1)} %slab.1.own_ref), channel_id=1, source_target_pairs={{480,0},{64,32},{32,64},{128,96},{96,128},{192,160},{160,192},{256... | collective-permute-start | bytes 393224 | tf_op jit(solution)/shard_map/ppermute | solution.py:350
  33.3 11.4 %collective-permute-start = (bf16[16,32,128]{2,1,0:T(8,128)(2,1)S(1)}, bf16[16,32,128]{2,1,0:T(8,128)(2,1)S(1)}, u32[]{:S(2)}, u32[]{:S(2)}) collective-permute-start(bf16[16,32,128]{2,1,0:T(8,128)(2,1)S(1)} %slab.1.own_ref), channel_id=1, source_target_pairs={{32,0},{0,32},{96,64},{64,96},{160,128},{128,160},{224,192},{192,2... | collective-permute-start | bytes 393224 | tf_op jit(solution)/shard_map/ppermute | solution.py:350
  35.2 11.4 %collective-permute-start.2 = (bf16[16,32,128]{2,1,0:T(8,128)(2,1)S(1)}, bf16[16,32,128]{2,1,0:T(8,128)(2,1)S(1)}, u32[]{:S(2)}, u32[]{:S(2)}) collective-permute-start(bf16[16,32,128]{2,1,0:T(8,128)(2,1)S(1)} %slab.1.own_ref), channel_id=1, source_target_pairs={{480,0},{448,32},{416,64},{384,96},{352,128},{320,160},{288,192},{... | collective-permute-start | bytes 393224 | tf_op jit(solution)/shard_map/ppermute | solution.py:350
  37.7 8.9 %collective-permute-start.3 = (bf16[16,32,128]{2,1,0:T(8,128)(2,1)S(1)}, bf16[16,32,128]{2,1,0:T(8,128)(2,1)S(1)}, u32[]{:S(2)}, u32[]{:S(2)}) collective-permute-start(bf16[16,32,128]{2,1,0:T(8,128)(2,1)S(1)} %slab.1.own_ref), channel_id=1, source_target_pairs={{0,0},{416,32},{448,64},{352,96},{384,128},{288,160},{320,192},{22... | collective-permute-start | bytes 393224 | tf_op jit(solution)/shard_map/ppermute | solution.py:350
  42.1 11.1 %collective-permute-start.4 = (bf16[16,32,128]{2,1,0:T(8,128)(2,1)S(1)}, bf16[16,32,128]{2,1,0:T(8,128)(2,1)S(1)}, u32[]{:S(2)}, u32[]{:S(2)}) collective-permute-start(bf16[16,32,128]{2,1,0:T(8,128)(2,1)S(1)} %collective-permute-done.1.next1_ref), channel_id=1, source_target_pairs={{416,0},{0,32},{352,64},{448,96},{288,128},{384,160},{224,192},{32... | collective-permute-start | bytes 393224 | tf_op jit(solution)/shard_map/ppermute | solution.py:350
  46.6 6.6 %copy-start = (s32[1,128]{1,0:T(1,128)S(1)}, s32[1,128]{1,0:T(1,128)}, u32[]{:S(2)}) copy-start(s32[1,128]{1,0:T(1,128)} %acquired_ref.1) | copy-start | bytes 1540

commit v6 on v4

--- a/solution.py
+++ b/solution.py
@@ -248,55 +248,41 @@
             ]
 
 
-def at(row, v):
-    return lambda d: pl.multiple_of(((row * SHIFTS + d) * 2 + v) * SC, SC)
-
-
-def early_kernel(own_ref, next0_ref, next1_ref, moves_ref, source_ref):
+def early_kernel(
+    own_ref, next0_ref, next1_ref, near_ref, weight_ref, moves_ref, sums_ref,
+    source_ref,
+):
+    straight, mirrored = moves_ref[0], moves_ref[1]
     odd = lax.axis_index("kz") % 2
+
+    def at(row, v):
+        return lambda d: pl.multiple_of(((row * SHIFTS + d) * 2 + v) * SC, SC)
+
     first, last = 2 * odd, 2 - 2 * odd
     for d in range(SHIFTS):
         for pair in range(NXL // 2):
             source_ref[pair, pl.ds(at(last, 1)(d), SC), :] = jnp.zeros((SC, 2 * NY3), BF16)
-    spread(source_ref, own_ref[...], moves_ref[0], at(1, 0))
-    spread(source_ref, next1_ref[...], moves_ref[0], at(first, 0))
-    spread(source_ref, next0_ref[...], moves_ref[0], at(last, 0))
-
-
-def middle_kernel(near_ref, weight_ref, moves_ref, _, sums_ref, source_ref):
-    spread(source_ref, near_ref[0], moves_ref[1], at(2 * (lax.axis_index("kz") % 2), 1))
-    spread(source_ref, near_ref[1], moves_ref[1], at(1, 1))
+    spread(source_ref, own_ref[...], straight, at(1, 0))
+    spread(source_ref, next1_ref[...], straight, at(first, 0))
+    spread(source_ref, near_ref[0], mirrored, at(first, 1))
+    spread(source_ref, near_ref[1], mirrored, at(1, 1))
+    spread(source_ref, next0_ref[...], straight, at(last, 0))
     weights = weight_ref[:, :KDIM]
     for pair in range(NXL // 2):
         sums_ref[pair] = dot(weights, source_ref[pair])
 
 
-def early(slabs, near, weights, moves):
-    vmem = pl.BlockSpec(memory_space=pltpu.VMEM)
-    source = jax.ShapeDtypeStruct((NXL // 2, KDIM, 2 * NY3), BF16)
-    spread_out = pl.pallas_call(
+def early(slabs, weights, moves):
+    return pl.pallas_call(
         early_kernel,
-        out_shape=source,
-        in_specs=[vmem] * 4,
-        out_specs=vmem,
-        compiler_params=room(12),
+        out_shape=jax.ShapeDtypeStruct((NXL // 2, 8 * SC, 2 * NY3), F32),
+        scratch_shapes=[pltpu.VMEM((NXL // 2, KDIM, 2 * NY3), BF16)],
+        compiler_params=room(16),
         cost_estimate=pl.CostEstimate(
-            flops=500_000_000, bytes_accessed=4_000_000, transcendentals=0
+            flops=1_500_000_000, bytes_accessed=4_000_000, transcendentals=0
         ),
         name="early",
-    )(*slabs, moves)
-    return pl.pallas_call(
-        middle_kernel,
-        out_shape=(jax.ShapeDtypeStruct((NXL // 2, 8 * SC, 2 * NY3), F32), source),
-        in_specs=[vmem] * 4,
-        out_specs=(vmem, vmem),
-        input_output_aliases={3: 1},
-        compiler_params=room(16),
-        cost_estimate=pl.CostEstimate(
-            flops=1_000_000_000, bytes_accessed=4_000_000, transcendentals=0
-        ),
-        name="middle",
-    )(near, weights, moves, spread_out)[0]
+    )(*slabs, weights, moves)
 
 
 def late_kernel(
@@ -373,7 +359,7 @@
     near = fetch(jnp.stack([own, next1]), lambda b: NZC - 2 * (b % 2) - b)
     far0 = fetch(next1[: NXL // 2], lambda b: NZC - 3 + 4 * (b % 2) - b)
     far1 = fetch(next1[NXL // 2 :], lambda b: NZC - 3 + 4 * (b % 2) - b)
-    sums = early((own, next0, next1), near, weights, moves)
+    sums = early((own, next0, next1, near), weights, moves)
     first = late(0, (), sums, far0, far_weights, moves, weave, acquired_at)
     return late(1, (first,), sums, far1, far_weights, moves, weave, acquired_at)
 

time: 56.3 us -> 62.1 us (1.10)
  waiting for transfers between devices: 8.52 us -> 13.9 us
    ppermute x5, waiting for transfers between devices: 3.83 us -> 9.2 us  [fetch(): return lax.ppermute(values, 'kz', pairs)]
    pallas_call x2 -> x1, Pallas kernels: 2.39 us -> 2.37 us  [early(): pl.pallas_call(early_kernel, out_shape=jax.ShapeDtypeStruct((NXL // 2, 8...]
  transfers between devices with their start and end apart: 6 -> 6, of which waited for: 2 -> 5; matrix products, arithmetic and copies ran while one was open for 0% -> 0% of each run, Pallas kernels for 12% -> 11%
where the time goes in v6:
time: 62.1 us; the launch traced here: 61.1 us
  starting transfers between devices  33.7 us (54%)
  waiting for transfers between devices  13.9 us (22%)
  Pallas kernels  11.1 us (18%)
  local copies, waits for them, and re-layouts  2.28 us (4%)
    ppermute x5, starting transfers between devices, fetch(): return lax.ppermute(values, 'kz', pairs)  23.2 us
    all_to_all x1, starting transfers between devices, local(): lax.all_to_all(spectra, 'gx', split_axis=0, concat_axis=0, tiled=True)  10.6 us
    ppermute x5, waiting for transfers between devices, fetch(): return lax.ppermute(values, 'kz', pairs)  9.2 us
    all_to_all x1, waiting for transfers between devices, local(): lax.all_to_all(spectra, 'gx', split_axis=0, concat_axis=0, tiled=True)  4.69 us
    pallas_call x2, Pallas kernels, late(): pl.pallas_call(functools.partial(late_kernel, half * NXL // 4), out_shape...  3.91 us
    pallas_call x1, Pallas kernels, early(): pl.pallas_call(early_kernel, out_shape=jax.ShapeDtypeStruct((NXL // 2, 8...  2.37 us
    unnamed x8, local copies, waits for them, and re-layouts  2.27 us
    pallas_call x1, Pallas kernels, placed_weights(): pl.pallas_call(weights_kernel, out_shape=(jax.ShapeDtypeStruct((8 * SC, K...  2.26 us
  transfers between devices with their start and end apart: 6, of which 5 were waited for; matrix products, arithmetic and copies ran while one was open for 0% of the time, Pallas kernels for 11%

profile of v6, /device:TPU:1, one launch (start us, length us, event | category | flops | bytes accessed | tf_op | source)
XLA Modules:
  0.0 61.1 jit_solution(5573959387961097428)
XLA Ops:
  0.0 2.1 %dft.1 = bf16[32,16,128]{2,1,0:T(8,128)(2,1)} custom-call(bf16[16,1,4,2,512]{4,3,2,1,0:T(2,128)(2,1)} %lines_hbm.1, bf16[256,512]{1,0:T(8,128)(2,1)} %constant.5.table_hbm), custom_call_target="tpu_custom_call" | custom-call | tf_op jit(solution)/shard_map/dft/pallas_call | solution.py:99
  2.1 10.6 %all-to-all-start = ((bf16[32,16,128]{2,1,0:T(8,128)(2,1)}), bf16[32,16,128]{2,1,0:T(8,128)(2,1)S(1)}, u32[]{:S(2)}, u32[]{:S(2)}) async-start(bf16[32,16,128]{2,1,0:T(8,128)(2,1)} %dft.1), calls=%async_computation | async-start | bytes 262144 | tf_op jit(solution)/shard_map/all_to_all | solution.py:347
  12.7 0.0 copy-start.1
  12.7 1.0 %copy-done.1 = bf16[2,6,16,6,32]{4,2,3,1,0:T(8,128)(2,1)S(1)} copy-done((bf16[2,6,16,6,32]{4,2,3,1,0:T(8,128)(2,1)S(1)}, bf16[2,6,16,6,32]{4,2,3,1,0:T(8,128)(2,1)}, u32[]{:S(2)}) %copy-start.1) | copy-done | bytes 73752
  13.7 0.0 copy-start.2
  13.7 0.7 %copy-done.2 = s32[6]{0:T(128)S(1)} copy-done((s32[6]{0:T(128)S(1)}, s32[6]{0:T(128)}, u32[]{:S(2)}) %copy-start.2) | copy-done | bytes 48
  14.3 0.0 copy-start.3
  14.3 0.7 %copy-done.3 = s32[6]{0:T(128)S(1)} copy-done((s32[6]{0:T(128)S(1)}, s32[6]{0:T(128)}, u32[]{:S(2)}) %copy-start.3) | copy-done | bytes 48
  15.0 2.3 %weights.1 = (bf16[256,1024]{1,0:T(8,128)(2,1)S(1)}, bf16[192,160]{1,0:T(8,128)(2,1)S(1)}, bf16[512,512]{1,0:T(8,128)(2,1)S(1)}, bf16[2,128,640]{2,1,0:T(8,128)(2,1)S(1)}, bf16[384,384]{1,0:T(8,128)(2,1)S(1)}) custom-call(s32[6]{0:T(128)S(1)} %copy-done.2, s32[6]{0:T(128)S(1)} %copy-done.3, bf16[2,6,6,16,32]{4,3,2,1,0:T(8,128)(2,1)S(1)} %bitcast.5), custom_call_target="tpu_custom_call" | custom-call | flops 100000000 | bytes 4000000 | tf_op jit(solution)/shard_map/weights/pallas_call | solution.py:220
  17.3 4.7 %all-to-all-done.in_ref = bf16[32,16,128]{2,1,0:T(8,128)(2,1)S(1)} async-done(((bf16[32,16,128]{2,1,0:T(8,128)(2,1)}), bf16[32,16,128]{2,1,0:T(8,128)(2,1)S(1)}, u32[]{:S(2)}, u32[]{:S(2)}) %all-to-all-start) | async-done | bytes 131104 | tf_op jit(solution)/shard_map/all_to_all | solution.py:347
  21.9 0.4 slab.1.own_ref
  22.3 11.9 %collective-permute-start.1 = (bf16[16,32,128]{2,1,0:T(8,128)(2,1)S(1)}, bf16[16,32,128]{2,1,0:T(8,128)(2,1)S(1)}, u32[]{:S(2)}, u32[]{:S(2)}) collective-permute-start(bf16[16,32,128]{2,1,0:T(8,128)(2,1)S(1)} %slab.1.own_ref), channel_id=1, source_target_pairs={{480,0},{64,32},{32,64},{128,96},{96,128},{192,160},{160,192},{256... | collective-permute-start | bytes 393224 | tf_op jit(solution)/shard_map/ppermute | solution.py:355
  34.3 5.7 %collective-permute-done.1.next1_ref = bf16[16,32,128]{2,1,0:T(8,128)(2,1)S(1)} collective-permute-done((bf16[16,32,128]{2,1,0:T(8,128)(2,1)S(1)}, bf16[16,32,128]{2,1,0:T(8,128)(2,1)S(1)}, u32[]{:S(2)}, u32[]{:S(2)}) %collective-permute-start.1) | collective-permute-done | bytes 131104 | tf_op jit(solution)/shard_map/ppermute | solution.py:355
  40.1 0.7 %collective-permute-start.2 = (bf16[2,16,32,128]{3,2,1,0:T(8,128)(2,1)S(1)}, bf16[2,16,32,128]{3,2,1,0:T(8,128)(2,1)S(1)}, u32[]{:S(2)}, u32[]{:S(2)}) collective-permute-start(bf16[2,16,32,128]{3,2,1,0:T(8,128)(2,1)S(1)} %pad_maximum_fusion), channel_id=1, source_target_pairs={{0,0},{416,32},{448,64},{352,96},{384,128},{288,160},{320,192},{22... | collective-permute-start | bytes 786440 | tf_op jit(solution)/shard_map/ppermute | solution.py:355
  40.8 4.4 %collective-permute-start = (bf16[16,32,128]{2,1,0:T(8,128)(2,1)S(1)}, bf16[16,32,128]{2,1,0:T(8,128)(2,1)S(1)}, u32[]{:S(2)}, u32[]{:S(2)}) collective-permute-start(bf16[16,32,128]{2,1,0:T(8,128)(2,1)S(1)} %slab.1.own_ref), channel_id=1, source_target_pairs={{32,0},{0,32},{96,64},{64,96},{160,128},{128,160},{224,192},{192,2... | collective-permute-start | bytes 393224 | tf_op jit(solution)/shard_map/ppermute | solution.py:355
  45.2 1.9 %collective-permute-start.4 = (bf16[8,32,128]{2,1,0:T(8,128)(2,1)S(1)}, bf16[8,32,128]{2,1,0:T(8,128)(2,1)S(1)}, u32[]{:S(2)}, u32[]{:S(2)}) collective-permute-start(bf16[8,32,128]{2,1,0:T(8,128)(2,1)S(1)} %get-tuple-element.15), channel_id=1, source_target_pairs={{416,0},{0,32},{352,64},{448,96},{288,128},{384,160},{224,192},{32... | collective-permute-start | bytes 196616 | tf_op jit(solution)/shard_map/ppermute | solution.py:355
  47.2 4.2 %collective-permute-start.3 = (bf16[8,32,128]{2,1,0:T(8,128)(2,1)S(1)}, bf16[8,32,128]{2,1,0:T(8,128)(2,1)S(1)}, u32[]{:S(2)}, u32[]{:S(2)}) collective-permute-start(bf16[8,32,128]{2,1,0:T(8,128)(2,1)S(1)} %get-tuple-element.16), channel_id=1, source_target_pairs={{416,0},{0,32},{352,64},{448,96},{288,128},{384,160},{224,192},{32... | collective-permute-start | bytes 196616 | tf_op jit(solution)/shard_map/ppermute | solution.py:355
  51.3 0.9 %collective-permute-done.next0_ref = bf16[16,32,128]{2,1,0:T(8,128)(2,1)S(1)} collective-permute-done((bf16[16,32,128]{2,1,0:T(8,128)(2,1)S(1)}, bf16[16,32,128]{2,1,0:T(8,128)(2,1)S(1)}, u32[]{:S(2)}, u32[]{:S(2)}) %collective-permute-start) | collective-permute-done | bytes 131104 | tf_op jit(solution)/shard_map/ppermute | solution.py:355
  52.2 0.0 collective-permute-done.2.near_ref
  52.2 0.0 copy-start
  52.2 2.4 %early.1.sums_ref = f32[8,256,256]{2,1,0:T(8,128)S(1)} custom-call(bf16[16,32,128]{2,1,0:T(8,128)(2,1)S(1)} %slab.1.own_ref, bf16[16,32,128]{2,1,0:T(8,128)(2,1)S(1)} %collective-permute-done.next0_ref, bf16[16,32,128]{2,1,0:T(8,128)(2,1)S(1)} %collective-permute-done.1.next1_ref, bf16[2,16,32,128]{3,2,1,0:T(8,128)(2,1)S(1)} %collective-permute-done.2.near_ref, ...), custom_call_target="tpu_custom_call" | custom-call | flops 1500000000 | bytes 4000000 | tf_op jit(solution)/shard_map/early/pallas_call | solution.py:276
  54.6 2.4 %collective-permute-done.4.far_ref = bf16[8,32,128]{2,1,0:T(8,128)(2,1)S(1)} collective-permute-done((bf16[8,32,128]{2,1,0:T(8,128)(2,1)S(1)}, bf16[8,32,128]{2,1,0:T(8,128)(2,1)S(1)}, u32[]{:S(2)}, u32[]{:S(2)}) %collective-permute-start.4) | collective-permute-done | bytes 65568 | tf_op jit(solution)/shard_map/ppermute | solution.py:355
  57.0 0.0 copy-done
  57.0 2.0 %shard_map.64.rest_0_ = bf16[2,16,16,2,384]{4,3,2,1,0:T(2,128)(2,1)} custom-call(f32[8,256,256]{2,1,0:T(8,128)S(1)} %early.1.sums_ref, bf16[8,32,128]{2,1,0:T(8,128)(2,1)S(1)} %collective-permute-done.4.far_ref, bf16[192,160]{1,0:T(8,128)(2,1)S(1)} %get-tuple-element.13.weight_ref, bf16[2,128,640]{2,1,0:T(8,128)(2,1)S(1)} %get-tuple-element.12.moves_ref, ...), custom_call_target="tpu_custom_call" | custom-call | tf_op jit(solution)/shard_map/pallas_call | solution.py:330
  59.0 0.1 collective-permute-done.3.far_ref
  59.1 2.0 %shard_map.65 = bf16[2,16,16,2,384]{4,3,2,1,0:T(2,128)(2,1)} custom-call(f32[8,256,256]{2,1,0:T(8,128)S(1)} %early.1.sums_ref, bf16[8,32,128]{2,1,0:T(8,128)(2,1)S(1)} %collective-permute-done.3.far_ref, bf16[192,160]{1,0:T(8,128)(2,1)S(1)} %get-tuple-element.13.weight_ref, ...), custom_call_target="tpu_custom_call", output_to_operand_aliasing={{}: (6, {})} | custom-call | tf_op jit(solution)/shard_map/pallas_call | solution.py:330
  (2 shorter events, 0.0 us)
Async XLA Ops:
  2.1 19.8 %all-to-all-start = ((bf16[32,16,128]{2,1,0:T(8,128)(2,1)}), bf16[32,16,128]{2,1,0:T(8,128)(2,1)S(1)}, u32[]{:S(2)}, u32[]{:S(2)}) async-start(bf16[32,16,128]{2,1,0:T(8,128)(2,1)} %dft.1), calls=%async_computation | async-start | bytes 262144 | tf_op jit(solution)/shard_map/all_to_all | solution.py:347
  12.7 1.0 %copy-start.1 = (bf16[2,6,16,6,32]{4,2,3,1,0:T(8,128)(2,1)S(1)}, bf16[2,6,16,6,32]{4,2,3,1,0:T(8,128)(2,1)}, u32[]{:S(2)}) copy-start(bf16[2,6,16,6,32]{4,2,3,1,0:T(8,128)(2,1)} %param.10) | copy-start | bytes 221188
  13.7 0.7 %copy-start.2 = (s32[6]{0:T(128)S(1)}, s32[6]{0:T(128)}, u32[]{:S(2)}) copy-start(s32[6]{0:T(128)} %ky_ref.1) | copy-start | bytes 76
  14.3 0.7 %copy-start.3 = (s32[6]{0:T(128)S(1)}, s32[6]{0:T(128)}, u32[]{:S(2)}) copy-start(s32[6]{0:T(128)} %kz_ref.1) | copy-start | bytes 76
  22.3 17.7 %collective-permute-start.1 = (bf16[16,32,128]{2,1,0:T(8,128)(2,1)S(1)}, bf16[16,32,128]{2,1,0:T(8,128)(2,1)S(1)}, u32[]{:S(2)}, u32[]{:S(2)}) collective-permute-start(bf16[16,32,128]{2,1,0:T(8,128)(2,1)S(1)} %slab.1.own_ref), channel_id=1, source_target_pairs={{480,0},{64,32},{32,64},{128,96},{96,128},{192,160},{160,192},{256... | collective-permute-start | bytes 393224 | tf_op jit(solution)/shard_map/ppermute | solution.py:355
  40.1 12.1 %collective-permute-start.2 = (bf16[2,16,32,128]{3,2,1,0:T(8,128)(2,1)S(1)}, bf16[2,16,32,128]{3,2,1,0:T(8,128)(2,1)S(1)}, u32[]{:S(2)}, u32[]{:S(2)}) collective-permute-start(bf16[2,16,32,128]{3,2,1,0:T(8,128)(2,1)S(1)} %pad_maximum_fusion), channel_id=1, source_target_pairs={{0,0},{416,32},{448,64},{352,96},{384,128},{288,160},{320,192},{22... | collective-permute-start | bytes 786440 | tf_op jit(solution)/shard_map/ppermute | solution.py:355
  40.8 11.5 %collective-permute-start = (bf16[16,32,128]{2,1,0:T(8,128)(2,1)S(1)}, bf16[16,32,128]{2,1,0:T(8,128)(2,1)S(1)}, u32[]{:S(2)}, u32[]{:S(2)}) collective-permute-start(bf16[16,32,128]{2,1,0:T(8,128)(2,1)S(1)} %slab.1.own_ref), channel_id=1, source_target_pairs={{32,0},{0,32},{96,64},{64,96},{160,128},{128,160},{224,192},{192,2... | collective-permute-start | bytes 393224 | tf_op jit(solution)/shard_map/ppermute | solution.py:355
  45.2 11.8 %collective-permute-start.4 = (bf16[8,32,128]{2,1,0:T(8,128)(2,1)S(1)}, bf16[8,32,128]{2,1,0:T(8,128)(2,1)S(1)}, u32[]{:S(2)}, u32[]{:S(2)}) collective-permute-start(bf16[8,32,128]{2,1,0:T(8,128)(2,1)S(1)} %get-tuple-element.15), channel_id=1, source_target_pairs={{416,0},{0,32},{352,64},{448,96},{288,128},{384,160},{224,192},{32... | collective-permute-start | bytes 196616 | tf_op jit(solution)/shard_map/ppermute | solution.py:355
  47.2 12.0 %collective-permute-start.3 = (bf16[8,32,128]{2,1,0:T(8,128)(2,1)S(1)}, bf16[8,32,128]{2,1,0:T(8,128)(2,1)S(1)}, u32[]{:S(2)}, u32[]{:S(2)}) collective-permute-start(bf16[8,32,128]{2,1,0:T(8,128)(2,1)S(1)} %get-tuple-element.16), channel_id=1, source_target_pairs={{416,0},{0,32},{352,64},{448,96},{288,128},{384,160},{224,192},{32... | collective-permute-start | bytes 196616 | tf_op jit(solution)/shard_map/ppermute | solution.py:355
  52.2 4.8 %copy-start = (s32[1,128]{1,0:T(1,128)S(1)}, s32[1,128]{1,0:T(1,128)}, u32[]{:S(2)}) copy-start(s32[1,128]{1,0:T(1,128)} %acquired_ref.3) | copy-start | bytes 1540
